TPU v7x, 32 devices: a whole 2x2x4 slice. The times are simulated.
32 devices in a mesh: front: 8 (over y, x, core), tile: 4 (over z).
Axes of the slice: x: 2, y: 2, z: 4, core: 2. Of those that a mesh axis runs over, the one named last changes fastest.
Arguments:
- pivot_inverse: float32 [8, 2, 512, 512], P('front', None, 'tile'), may hold values from -0.26516504 to 0.26516504
- panel_upper: float32 [8, 2, 512, 2048], P('front', None, None, 'tile'), may hold values from -6 to 6
- panel_lower: float32 [8, 2, 2048, 512], P('front', None, 'tile'), may hold values from -4.2426407 to 4.2426407
- index_map: int32 [8, 2, 2048], replicated, may hold values from 0 to 4095, as said below
- parent_base: float32 [8, 4096, 4096], P('front', None, 'tile'), may hold values from -512 to 512
Outputs:
- parent_front: float32 [8, 4096, 4096], P('front', None, 'tile')
Inputs may be any that keep to these rules, and one draw needn't show every extreme that they name: Each list index_map[g, c] holds 2048 distinct parent indices in no particular order, among them 0 and 4095.
All inputs are finite; a program needn't handle non-finite values.
Results may differ from a plain program's by a relative error of at most 0.0003.
Values sent between devices are 32-bit elements; how exact they have to be, the bound alone decides.
A program may use at most 128 MiB of HBM per device.

v0:
```python
import functools

import jax
import jax.numpy as jnp
from jax import lax
from jax.experimental import pallas as pl
from jax.experimental.pallas import tpu as pltpu
from jax.sharding import PartitionSpec as P

MESH = pl.DeviceIdType.MESH


def parts(value):
    high = value.astype(jnp.bfloat16)
    return high, (value - high.astype(jnp.float32)).astype(jnp.bfloat16)


def dot(left, right, contract=(1, 0)):
    dims = (((contract[0],), (contract[1],)), ((), ()))
    return lax.dot_general(left, right, dims, preferred_element_type=jnp.float32)


def split_product(left, right):
    total = dot(left[0], right[0])
    total = total + dot(left[0], right[1])
    return total + dot(left[1], right[0])


def update_kernel(
    n, inv_in, up_in, low_in, map_ref, u_out, index_out,
    up, inv, low, up_h, up_l, inv_h, inv_l, f_end, f_own, f_h, f_l, stage,
    local_sem, part_send, part_recv, up_send, up_recv, inv_send, inv_recv,
    low_send, low_recv, f_send, f_recv, out_sem,
):
    t = lax.axis_index("tile")
    f = lax.axis_index("front")
    partner = lax.rem(f, 2) * -2 + 1 + f
    count = map_ref.shape[2]
    wc = up.shape[3]
    kr = inv.shape[2]
    width = f_own.shape[2]
    chunk = min(256, width)
    middle = (t >= 1) & (t <= n - 2)
    at_end = (t == 0) | (t == n - 1)

    barrier = pltpu.get_barrier_semaphore()
    pl.semaphore_signal(barrier, inc=1, device_id=(partner, t), device_id_type=MESH)

    @pl.when(t > 0)
    def _():
        pl.semaphore_signal(barrier, inc=1, device_id=(f, t - 1), device_id_type=MESH)

    @pl.when(t < n - 1)
    def _():
        pl.semaphore_signal(barrier, inc=1, device_id=(f, t + 1), device_id_type=MESH)

    @pl.when(at_end)
    def _():
        pl.semaphore_wait(barrier, 2)

    @pl.when(middle)
    def _():
        pl.semaphore_wait(barrier, 3)

    sources = (up_in, inv_in, low_in)
    targets = (up, inv, low)

    def local(kind):
        return pltpu.make_async_copy(sources[kind].at[0], targets[kind].at[0, t], local_sem.at[kind])

    def exchange(kind):
        return pltpu.make_async_remote_copy(
            src_ref=sources[kind].at[1], dst_ref=targets[kind].at[1, t],
            send_sem=part_send.at[kind], recv_sem=part_recv.at[kind],
            device_id=(partner, t), device_id_type=MESH,
        )

    def hop(kind, child, shard, side):
        send, recv = ((up_send, up_recv), (inv_send, inv_recv), (low_send, low_recv))[kind]
        ref = targets[kind].at[child, shard]
        return pltpu.make_async_remote_copy(
            src_ref=ref, dst_ref=ref,
            send_sem=send.at[side, child, shard], recv_sem=recv.at[child, shard],
            device_id=(f, lax.rem(t + (1 if side == 0 else n - 1), n)), device_id_type=MESH,
        )

    def takes(kind, side):
        if kind == 2:
            return t + 1 <= n - 1 if side == 0 else t - 1 >= 0
        return t + 1 <= n - 2 if side == 0 else t - 1 >= 1

    def send(kind, child, shard, side):
        @pl.when(takes(kind, side))
        def _():
            hop(kind, child, shard, side).start()

    def send_own(kind, child):
        send(kind, child, t, 0)
        send(kind, child, t, 1)

    def relay(kinds, child, d):
        for side, shard, valid in ((0, t - d, t - d >= 0), (1, t + d, t + d <= n - 1)):
            @pl.when(valid & (middle if 0 in kinds else t >= 0))
            def _():
                for kind in kinds:
                    hop(kind, child, shard, side).wait_recv()
                    send(kind, child, shard, side)

    def split_child(child):
        @pl.loop(0, n)
        def _(s):
            high, low_part = parts(up[child, s])
            up_h[s] = high
            up_l[s] = low_part
            rows = pl.ds(pl.multiple_of(s * kr, kr), kr)
            high, low_part = parts(inv[child, s])
            inv_h[rows, :] = high
            inv_l[rows, :] = low_part

    def factor(child, start, dst, after):
        @pl.loop(0, width // chunk)
        def _(j):
            base = pl.multiple_of(j * chunk, chunk)
            columns = lax.broadcasted_iota(jnp.int32, (chunk, wc), 0) + (start + base)
            high = low_part = None
            for s in range(n):
                listed = map_ref[child, :, s * wc:(s + 1) * wc]
                choose = (columns == listed).astype(jnp.float32).astype(jnp.bfloat16)
                a = dot(up_h[s], choose, (1, 1))
                b = dot(up_l[s], choose, (1, 1))
                high = a if high is None else high + a
                low_part = b if low_part is None else low_part + b
            picked = (high.astype(jnp.bfloat16), low_part.astype(jnp.bfloat16))
            dst[child, :, pl.ds(base, chunk)] = split_product((inv_h[...], inv_l[...]), picked)
            after(j)

    def end_copy(child, j, target):
        cols = pl.ds(pl.multiple_of(j * chunk, chunk), chunk)
        return pltpu.make_async_remote_copy(
            src_ref=f_end.at[child, :, cols], dst_ref=f_own.at[child, :, cols],
            send_sem=f_send.at[child, j], recv_sem=f_recv.at[child, j],
            device_id=(f, target), device_id_type=MESH,
        )

    server = (t == 1) | (t == n - 2)
    end = lax.div(t - 1, n - 3) * (n - 1)
    aside = lax.rem(t + 1, n)

    def serve(child):
        @pl.when(middle)
        def _():
            split_child(child)

            @pl.when(server)
            def _():
                factor(child, end * width, f_end, lambda j: end_copy(child, j, end).start())

            factor(child, t * width, f_own, lambda j: None)

    def split_factor(child):
        @pl.when(at_end)
        def _():
            @pl.loop(0, width // chunk)
            def _(j):
                end_copy(child, j, aside).wait_recv()

        @pl.loop(0, width // chunk)
        def _(j):
            cols = pl.ds(pl.multiple_of(j * chunk, chunk), chunk)
            high, low_part = parts(f_own[child, :, cols])
            f_h[child, :, cols] = high
            f_l[child, :, cols] = low_part

    lr = low.shape[2]
    tall = stage.shape[0] // lr

    def put(child, shard):
        left = parts(low[child, shard])

        @pl.loop(0, width // chunk)
        def _(j):
            cols = pl.ds(pl.multiple_of(j * chunk, chunk), chunk)
            block = split_product(left, (f_h[child, :, cols], f_l[child, :, cols]))
            for q in range(chunk // 128):
                strip = pl.ds(j * (chunk // 128) + q, lr, stride=tall)
                stage[strip, :] = block[:, q * 128:(q + 1) * 128]

        copy = pltpu.make_async_copy(stage, u_out.at[child, shard], out_sem)
        copy.start()
        copy.wait()

    def index_rows():
        shape = (8, count)
        place = lax.broadcasted_iota(jnp.int32, shape, 1)
        which = lax.broadcasted_iota(jnp.int32, shape, 0)
        digits = jnp.where(which == 0, place >> 7, jnp.where(which == 1, place & 127, 1))
        digits = digits.astype(jnp.float32).astype(jnp.bfloat16)
        span = min(256, index_out.shape[2])
        for child in range(2):
            @pl.loop(0, index_out.shape[2] // span)
            def _(j):
                base = pl.multiple_of(j * span, span)
                rows = lax.broadcasted_iota(jnp.int32, (span, count), 0) + base
                choose = (rows == map_ref[child]).astype(jnp.float32).astype(jnp.bfloat16)
                found = dot(digits, choose, (1, 1)).astype(jnp.int32)
                source = found[0:1] * 128 + found[1:2] + child * count
                index_out[child, :, pl.ds(base, span)] = jnp.where(found[2:3] > 0, source, 2 * count)

    for kind in range(3):
        exchange(kind).start()
        local(kind).start()
    for kind in range(3):
        local(kind).wait()
    send_own(0, 0)
    send_own(1, 0)

    @pl.when(t == n - 2)
    def _():
        hop(2, 0, t, 0).start()

    @pl.when(t == 1)
    def _():
        hop(2, 0, t, 1).start()

    for kind in range(3):
        exchange(kind).wait()

    @pl.when(t == n - 2)
    def _():
        hop(2, 1, t, 0).start()

    @pl.when(t == 1)
    def _():
        hop(2, 1, t, 1).start()

    index_rows()

    @pl.loop(1, n)
    def _(d):
        relay((0, 1), 0, d)

    send_own(0, 1)
    send_own(1, 1)
    serve(0)

    @pl.loop(1, n)
    def _(d):
        relay((0, 1), 1, d)

    for child in range(2):
        @pl.when((t < n - 1) & (t != n - 2))
        def _():
            hop(2, child, t, 0).start()

        @pl.when((t > 0) & (t != 1))
        def _():
            hop(2, child, t, 1).start()

    serve(1)
    for child in range(2):
        split_factor(child)

    @pl.loop(0, 2)
    def _(child):
        put(child, t)

    @pl.loop(1, n)
    def _(d):
        @pl.loop(0, 2)
        def _(child):
            relay((2,), child, d)

            @pl.when(t - d >= 0)
            def _():
                put(child, t - d)

            @pl.when(t + d <= n - 1)
            def _():
                put(child, t + d)

    for child in range(2):
        @pl.loop(0, n)
        def _(s):
            for side in range(2):
                for kind in range(3):
                    @pl.when(takes(kind, side) & (s <= t if side == 0 else s >= t))
                    def _():
                        hop(kind, child, s, side).wait_send()

        @pl.when(server)
        def _():
            @pl.loop(0, width // chunk)
            def _(j):
                end_copy(child, j, aside).wait_send()


def gathered_updates(inverse, upper, lower, maps, n, order, width):
    pivots = inverse.shape[2]
    kr, wc, lr = inverse.shape[1], upper.shape[2], lower.shape[1]
    vmem = pltpu.VMEM
    dma = pltpu.SemaphoreType.DMA
    f32, b16 = jnp.float32, jnp.bfloat16
    chunks = width // min(256, width)
    tall = -(-width // 1024) * 8
    return pl.pallas_call(
        functools.partial(update_kernel, n),
        out_shape=(
            jax.ShapeDtypeStruct((2, n, lr * tall, 128), f32),
            jax.ShapeDtypeStruct((2, 1, order), jnp.int32),
        ),
        in_specs=[pl.BlockSpec(memory_space=pl.ANY)] * 3 + [pl.BlockSpec(memory_space=vmem)],
        out_specs=(pl.BlockSpec(memory_space=pl.ANY), pl.BlockSpec(memory_space=vmem)),
        scratch_shapes=[
            vmem((2, n, pivots, wc), f32),
            vmem((2, n, kr, pivots), f32),
            vmem((2, n, lr, pivots), f32),
            vmem((n, pivots, wc), b16),
            vmem((n, pivots, wc), b16),
            vmem((n * kr, pivots), b16),
            vmem((n * kr, pivots), b16),
            vmem((2, pivots, width), f32),
            vmem((2, pivots, width), f32),
            vmem((2, pivots, width), b16),
            vmem((2, pivots, width), b16),
            vmem((lr * tall, 128), f32),
            dma((3,)), dma((3,)), dma((3,)),
            dma((2, 2, n)), dma((2, n)),
            dma((2, 2, n)), dma((2, n)),
            dma((2, 2, n)), dma((2, n)),
            dma((2, chunks)), dma((2, chunks)), dma,
        ],
        compiler_params=pltpu.CompilerParams(
            collective_id=0, has_side_effects=True, vmem_limit_bytes=56 * 1024 * 1024
        ),
    )(inverse, upper, lower, maps)


def place_kernel(index_ref, base_ref, u_ref, out_ref, u, rows, sem):
    block, width = base_ref.shape
    order = block * pl.num_programs(0)
    total = u_ref.shape[0]
    tall = rows.shape[0] // block
    start = pl.program_id(0) * block

    @pl.when(pl.program_id(0) == 0)
    def _():
        copy = pltpu.make_async_copy(u_ref, u.at[pl.ds(0, total)], sem)
        copy.start()
        u[pl.ds(total, tall), :] = jnp.zeros((tall, 128), jnp.float32)
        copy.wait()

    turn = 32

    @pl.loop(0, block // turn)
    def _(i):
        for j in range(turn):
            r = i * turn + j
            a = u[pl.ds(pl.multiple_of(index_ref[start + r] * tall, tall), tall), :]
            b = u[pl.ds(pl.multiple_of(index_ref[order + start + r] * tall, tall), tall), :]
            rows[pl.ds(pl.multiple_of(r * tall, tall), tall), :] = a + b

    for q in range(width // 128):
        cols = slice(q * 128, (q + 1) * 128)
        out_ref[:, cols] = base_ref[:, cols] - rows[pl.ds(q, block, stride=tall), :]


def placed(base, updates, index):
    order, width = base.shape
    block = min(256, order)
    tall = -(-width // 1024) * 8
    return pl.pallas_call(
        place_kernel,
        out_shape=jax.ShapeDtypeStruct(base.shape, base.dtype),
        grid_spec=pltpu.PrefetchScalarGridSpec(
            num_scalar_prefetch=1,
            grid=(order // block,),
            in_specs=[
                pl.BlockSpec((block, width), lambda i, *_: (i, 0)),
                pl.BlockSpec(memory_space=pl.ANY),
            ],
            out_specs=pl.BlockSpec((block, width), lambda i, *_: (i, 0)),
            scratch_shapes=[
                pltpu.VMEM((updates.shape[0] + tall, 128), jnp.float32),
                pltpu.VMEM((block * tall, 128), jnp.float32),
                pltpu.SemaphoreType.DMA,
            ],
        ),
        compiler_params=pltpu.CompilerParams(vmem_limit_bytes=40 * 1024 * 1024),
    )(index, base, updates)


def shards(pivot_inverse, panel_upper, panel_lower, index_map, parent_base):
    base = parent_base[0]
    order, width = base.shape
    n = lax.axis_size("tile")
    group = lax.axis_index("front")
    partner = jnp.bitwise_xor(group, 1)
    maps = jnp.stack([
        lax.dynamic_index_in_dim(index_map, group, 0, keepdims=False)[0],
        lax.dynamic_index_in_dim(index_map, partner, 0, keepdims=False)[1],
    ])
    updates, index = gathered_updates(
        pivot_inverse[0], panel_upper[0], panel_lower[0], maps[:, None, :], n, order, width
    )
    return placed(base, updates.reshape(-1, 128), index.reshape(-1))[None]


def solution(mesh):
    return jax.shard_map(
        shards,
        mesh=mesh,
        in_specs=(
            P("front", None, "tile", None),
            P("front", None, None, "tile"),
            P("front", None, "tile", None),
            P(),
            P("front", None, "tile"),
        ),
        out_specs=P("front", None, "tile"),
        check_vma=False,
    )
```

profile of v0, /device:TPU:0, one launch (start us, length us, event | category | flops | bytes accessed | tf_op | source)
XLA Modules:
  0.0 292.5 jit_solution(14982202948252297826)
XLA Ops:
  0.0 0.8 dynamic-slice_bitcast_fusion.1
  0.8 0.6 broadcast_in_dim.6.map_ref
  1.4 260.8 %shard_map.55 = (f32[2,4,4096,128]{3,2,1,0:T(8,128)}, s32[2,1,4096]{2,1,0:T(1,128)}) custom-call(f32[2,128,512]{2,1,0:T(8,128)} %bitcast.16, f32[2,512,512]{2,1,0:T(8,128)} %bitcast.14, f32[2,512,512]{2,1,0:T(8,128)} %bitcast.15, s32[2,1,2048]{2,1,0:T(1,128)} %broadcast_in_dim.6.map_ref), custom_call_target="tpu_custom_call" | custom-call | tf_op jit(solution)/shard_map/pallas_call | solution.py:305
  262.2 0.0 copy-start
  262.2 0.7 copy-done
  263.0 29.5 %shard_map.56 = f32[4096,1024]{1,0:T(8,128)} custom-call(s32[8192]{0:T(1024)S(1)} %bitcast.11, f32[4096,1024]{1,0:T(8,128)} %bitcast.12, f32[32768,128]{1,0:T(8,128)} %bitcast.13), custom_call_target="tpu_custom_call" | custom-call | tf_op jit(solution)/shard_map/pallas_call | solution.py:371
  (1 shorter events, 0.0 us)
Async XLA Ops:
  262.2 0.8 copy-start
where the time goes:
time: 293 us; the launch traced here: 292 us
  Pallas kernels  290 us (99%)
    pallas_call x1, Pallas kernels, gathered_updates(): pl.pallas_call(functools.partial(update_kernel, n), out_shape=(jax.ShapeD...  261 us
    pallas_call x1, Pallas kernels, placed(): pl.pallas_call(place_kernel, out_shape=jax.ShapeDtypeStruct(base.shape, b...  29.5 us

commit v1 on v0

v1 whole, which is shorter than its diff:
```python
import functools

import jax
import jax.numpy as jnp
from jax import lax
from jax.experimental import pallas as pl
from jax.experimental.pallas import tpu as pltpu
from jax.sharding import PartitionSpec as P

MESH = pl.DeviceIdType.MESH


def parts(value):
    high = value.astype(jnp.bfloat16)
    return high, (value - high.astype(jnp.float32)).astype(jnp.bfloat16)


def dot(left, right, contract=(1, 0)):
    dims = (((contract[0],), (contract[1],)), ((), ()))
    return lax.dot_general(left, right, dims, preferred_element_type=jnp.float32)


def one_hot(match):
    return match.astype(jnp.float32).astype(jnp.bfloat16)


def front_kernel(
    n, inv_in, up_in, low_in, map_ref, base_in, x_out,
    up, inv, low, up_h, up_l, inv_h, inv_l, low_h, low_l, lx_h, lx_l, f_buf, f_h, f_l, x_buf,
    local_sem, part_send, part_recv, up_send, up_recv, inv_send, inv_recv,
    low_send, low_recv, f_send, f_recv, in_sem, out_sem,
):
    t = lax.axis_index("tile")
    f = lax.axis_index("front")
    partner = lax.rem(f, 2) * -2 + 1 + f
    count = map_ref.shape[2]
    wc = up.shape[3]
    kr = inv.shape[2]
    lr = low.shape[2]
    order, width = x_out.shape
    chunk = min(256, width)
    chunks = width // chunk
    middle = (t >= 1) & (t <= n - 2)
    at_end = (t == 0) | (t == n - 1)
    lower = t < n // 2

    barrier = pltpu.get_barrier_semaphore()
    pl.semaphore_signal(barrier, inc=1, device_id=(partner, t), device_id_type=MESH)

    @pl.when(t > 0)
    def _():
        pl.semaphore_signal(barrier, inc=1, device_id=(f, t - 1), device_id_type=MESH)

    @pl.when(t < n - 1)
    def _():
        pl.semaphore_signal(barrier, inc=1, device_id=(f, t + 1), device_id_type=MESH)

    @pl.when(at_end)
    def _():
        pl.semaphore_wait(barrier, 2)

    @pl.when(middle)
    def _():
        pl.semaphore_wait(barrier, 3)

    sources = (up_in, inv_in, low_in)
    targets = (up, inv, low)

    def local(kind):
        return pltpu.make_async_copy(sources[kind].at[0], targets[kind].at[0, t], local_sem.at[kind])

    def exchange(kind):
        return pltpu.make_async_remote_copy(
            src_ref=sources[kind].at[1], dst_ref=targets[kind].at[1, t],
            send_sem=part_send.at[kind], recv_sem=part_recv.at[kind],
            device_id=(partner, t), device_id_type=MESH,
        )

    def hop(kind, child, shard, side):
        send, recv = ((up_send, up_recv), (inv_send, inv_recv), (low_send, low_recv))[kind]
        ref = targets[kind].at[child, shard]
        return pltpu.make_async_remote_copy(
            src_ref=ref, dst_ref=ref,
            send_sem=send.at[side, child, shard], recv_sem=recv.at[child, shard],
            device_id=(f, lax.rem(t + (1 if side == 0 else n - 1), n)), device_id_type=MESH,
        )

    def takes(kind, side):
        if kind == 2:
            return t + 1 <= n - 1 if side == 0 else t - 1 >= 0
        return t + 1 <= n - 2 if side == 0 else t - 1 >= 1

    def send(kind, child, shard, side):
        @pl.when(takes(kind, side))
        def _():
            hop(kind, child, shard, side).start()

    def send_own(kind, child):
        send(kind, child, t, 0)
        send(kind, child, t, 1)

    def pass_on(kinds, child, d, side, where):
        shard = t - d if side == 0 else t + d
        inside = shard >= 0 if side == 0 else shard <= n - 1

        @pl.when(inside & where)
        def _():
            for kind in kinds:
                hop(kind, child, shard, side).wait_recv()
                send(kind, child, shard, side)

    def relay_low(child, d):
        pass_on((2,), child, d, 0, t >= 0)
        pass_on((2,), child, d, 1, t >= 0)

    def near(child):
        @pl.loop(1, n)
        def _(d):
            pass_on((1, 0), child, d, 0, middle & lower)
            pass_on((1, 0), child, d, 1, middle & (t >= n // 2))

    def far(child):
        @pl.loop(1, n)
        def _(d):
            pass_on((1, 0), child, d, 1, middle & lower)
            pass_on((1, 0), child, d, 0, middle & (t >= n // 2))

    def place_rows(child):
        @pl.loop(0, n)
        def _(s):
            rows = pl.ds(pl.multiple_of(s * lr, lr), lr)
            high, low_part = parts(low[child, s])
            low_h[rows, :] = high
            low_l[rows, :] = low_part

        span = min(256, order)

        @pl.loop(0, order // span)
        def _(j):
            base = pl.multiple_of(j * span, span)
            rows = lax.broadcasted_iota(jnp.int32, (span, count), 0) + base
            choose = one_hot(rows == map_ref[child])
            lx_h[child, pl.ds(base, span), :] = dot(choose, low_h[...]).astype(jnp.bfloat16)
            lx_l[child, pl.ds(base, span), :] = dot(choose, low_l[...]).astype(jnp.bfloat16)

    def split_child(child):
        @pl.loop(0, n)
        def _(s):
            high, low_part = parts(up[child, s])
            up_h[s] = high
            up_l[s] = low_part
            rows = pl.ds(pl.multiple_of(s * kr, kr), kr)
            high, low_part = parts(inv[child, s])
            inv_h[rows, :] = high
            inv_l[rows, :] = low_part

    def factor(child, start, j):
        columns = lax.broadcasted_iota(jnp.int32, (chunk, wc), 0) + (start + j * chunk)
        high = low_part = None
        for s in range(n):
            choose = one_hot(columns == map_ref[child, :, s * wc:(s + 1) * wc])
            a = dot(choose, up_h[s], (1, 1))
            b = dot(choose, up_l[s], (1, 1))
            high = a if high is None else high + a
            low_part = b if low_part is None else low_part + b
        high = high.astype(jnp.bfloat16)
        low_part = low_part.astype(jnp.bfloat16)
        total = dot(high, inv_h[...], (1, 1))
        total = total + dot(low_part, inv_h[...], (1, 1))
        return total + dot(high, inv_l[...], (1, 1))

    def strip(j):
        return pl.ds(pl.multiple_of(j * chunk, chunk), chunk)

    def end_copy(child, j, target):
        ref = f_buf.at[child, strip(j)]
        return pltpu.make_async_remote_copy(
            src_ref=ref, dst_ref=ref,
            send_sem=f_send.at[child, j], recv_sem=f_recv.at[child, j],
            device_id=(f, target), device_id_type=MESH,
        )

    server = (t == 1) | (t == n - 2)
    end = lax.div(t - 1, n - 3) * (n - 1)
    aside = lax.rem(t + 1, n)

    def serve(child):
        @pl.when(middle)
        def _():
            split_child(child)

            @pl.when(server)
            def _():
                @pl.loop(0, chunks)
                def _(j):
                    f_buf[child, strip(j), :] = factor(child, end * width, j)
                    end_copy(child, j, end).start()

            @pl.loop(0, chunks)
            def _(j):
                high, low_part = parts(factor(child, t * width, j))
                f_h[child, strip(j), :] = high
                f_l[child, strip(j), :] = low_part

    def take_factor(child, j):
        @pl.when(at_end)
        def _():
            end_copy(child, j, aside).wait_recv()
            high, low_part = parts(f_buf[child, strip(j), :])
            f_h[child, strip(j), :] = high
            f_l[child, strip(j), :] = low_part

    slots = x_buf.shape[0]
    ahead = slots // 2
    tall = x_buf.shape[1]
    per = order // tall
    blocks = per * chunks

    def window(ref, i):
        rows = pl.ds(pl.multiple_of(lax.rem(i, per) * tall, tall), tall)
        return ref.at[rows, strip(lax.div(i, per))]

    def subtract(child):
        source = base_in if child == 0 else x_out

        def load(i):
            slot = lax.rem(i, slots)
            return pltpu.make_async_copy(window(source, i), x_buf.at[slot], in_sem.at[slot])

        def store(i):
            slot = lax.rem(i, slots)
            return pltpu.make_async_copy(x_buf.at[slot], window(x_out, i), out_sem.at[slot])

        for i in range(ahead):
            load(i).start()

        @pl.loop(0, blocks)
        def _(i):
            j = lax.div(i, per)

            @pl.when(lax.rem(i, per) == 0)
            def _():
                take_factor(child, j)

            @pl.when(i + ahead < blocks)
            def _():
                @pl.when(i >= slots - ahead)
                def _():
                    store(i - (slots - ahead)).wait()

                load(i + ahead).start()

            rows = pl.ds(pl.multiple_of(lax.rem(i, per) * tall, tall), tall)
            high = f_h[child, strip(j), :]
            left = lx_h[child, rows, :]
            total = dot(left, high, (1, 1))
            total = total + dot(left, f_l[child, strip(j), :], (1, 1))
            total = total + dot(lx_l[child, rows, :], high, (1, 1))
            load(i).wait()
            slot = lax.rem(i, slots)
            x_buf[slot] = x_buf[slot] - total
            store(i).start()

        for i in range(max(blocks - slots, 0), blocks):
            store(i).wait()

    for kind in (2, 1, 0):
        exchange(kind).start()
        local(kind).start()
    local(2).wait()
    send_own(2, 0)
    exchange(2).wait()
    send_own(2, 1)
    for kind in (1, 0):
        local(kind).wait()
        exchange(kind).wait()

    @pl.when(at_end)
    def _():
        for child in range(2):
            send_own(1, child)
            send_own(0, child)

    relay_low(0, 1)
    relay_low(1, 1)

    @pl.when(middle)
    def _():
        send_own(1, 0)
        send_own(0, 0)

    relay_low(0, 2)
    near(0)

    @pl.when(middle)
    def _():
        send_own(1, 1)
        send_own(0, 1)

    relay_low(1, 2)

    @pl.loop(3, n - 1)
    def _(d):
        relay_low(0, d)
        relay_low(1, d)

    relay_low(0, n - 1)
    place_rows(0)
    near(1)
    relay_low(1, n - 1)
    place_rows(1)
    far(0)
    serve(0)
    subtract(0)
    far(1)
    serve(1)
    subtract(1)

    for child in range(2):
        @pl.loop(0, n)
        def _(s):
            for side in range(2):
                for kind in range(3):
                    @pl.when(takes(kind, side) & (s <= t if side == 0 else s >= t))
                    def _():
                        hop(kind, child, s, side).wait_send()

        @pl.when(server)
        def _():
            @pl.loop(0, chunks)
            def _(j):
                end_copy(child, j, aside).wait_send()


def assembled(inverse, upper, lower, maps, base, n):
    order, width = base.shape
    pivots = inverse.shape[2]
    count = maps.shape[2]
    kr, wc, lr = inverse.shape[1], upper.shape[2], lower.shape[1]
    vmem = pltpu.VMEM
    dma = pltpu.SemaphoreType.DMA
    f32, b16 = jnp.float32, jnp.bfloat16
    chunk = min(256, width)
    chunks = width // chunk
    slots = 4
    whole = pl.BlockSpec(memory_space=pl.ANY)
    return pl.pallas_call(
        functools.partial(front_kernel, n),
        out_shape=jax.ShapeDtypeStruct((order, width), f32),
        in_specs=[whole] * 3 + [pl.BlockSpec(memory_space=vmem), whole],
        out_specs=whole,
        scratch_shapes=[
            vmem((2, n, pivots, wc), f32),
            vmem((2, n, kr, pivots), f32),
            vmem((2, n, lr, pivots), f32),
            vmem((n, pivots, wc), b16),
            vmem((n, pivots, wc), b16),
            vmem((n * kr, pivots), b16),
            vmem((n * kr, pivots), b16),
            vmem((count, pivots), b16),
            vmem((count, pivots), b16),
            vmem((2, order, pivots), b16),
            vmem((2, order, pivots), b16),
            vmem((2, width, pivots), f32),
            vmem((2, width, pivots), b16),
            vmem((2, width, pivots), b16),
            vmem((slots, min(1024, order), chunk), f32),
            dma((3,)), dma((3,)), dma((3,)),
            dma((2, 2, n)), dma((2, n)),
            dma((2, 2, n)), dma((2, n)),
            dma((2, 2, n)), dma((2, n)),
            dma((2, chunks)), dma((2, chunks)),
            dma((slots,)), dma((slots,)),
        ],
        compiler_params=pltpu.CompilerParams(
            collective_id=0, has_side_effects=True, vmem_limit_bytes=63 * 1024 * 1024
        ),
    )(inverse, upper, lower, maps, base)


def shards(pivot_inverse, panel_upper, panel_lower, index_map, parent_base):
    n = lax.axis_size("tile")
    group = lax.axis_index("front")
    partner = jnp.bitwise_xor(group, 1)
    maps = jnp.stack([
        lax.dynamic_index_in_dim(index_map, group, 0, keepdims=False)[0],
        lax.dynamic_index_in_dim(index_map, partner, 0, keepdims=False)[1],
    ])
    return assembled(
        pivot_inverse[0], panel_upper[0], panel_lower[0], maps[:, None, :], parent_base[0], n
    )[None]


def solution(mesh):
    return jax.shard_map(
        shards,
        mesh=mesh,
        in_specs=(
            P("front", None, "tile", None),
            P("front", None, None, "tile"),
            P("front", None, "tile", None),
            P(),
            P("front", None, "tile"),
        ),
        out_specs=P("front", None, "tile"),
        check_vma=False,
    )
```

time: 293 us -> 278 us (0.949)
  Pallas kernels: 290 us -> 265 us
  local copies, waits for them, and re-layouts: 2.12 us -> 13.3 us
    pallas_call x2 -> x1, Pallas kernels: 290 us -> 265 us  [assembled(): pl.pallas_call(functools.partial(front_kernel, n), out_shape=jax.ShapeDty...]
    unnamed x2 -> x1, local copies, waits for them, and re-layouts: 0.75 us -> 12 us
where the time goes in v1:
time: 278 us
  Pallas kernels  265 us (95%)
  local copies, waits for them, and re-layouts  13.3 us (5%)
    pallas_call x1, Pallas kernels, assembled(): pl.pallas_call(functools.partial(front_kernel, n), out_shape=jax.ShapeDty...  265 us
    unnamed x1, local copies, waits for them, and re-layouts  12 us

profile of v1, /device:TPU:0, one launch (start us, length us, event | category | flops | bytes accessed | tf_op | source)
XLA Modules:
  0.0 277.9 jit_solution(16949817473996415365)
XLA Ops:
  0.0 0.8 dynamic-slice_bitcast_fusion.1
  0.8 0.6 broadcast_in_dim.6.map_ref
  1.4 264.6 %shard_map.55 = f32[4096,1024]{1,0:T(8,128)} custom-call(f32[2,128,512]{2,1,0:T(8,128)} %bitcast.13, f32[2,512,512]{2,1,0:T(8,128)} %bitcast.11, f32[2,512,512]{2,1,0:T(8,128)} %bitcast.12, s32[2,1,2048]{2,1,0:T(1,128)} %broadcast_in_dim.6.map_ref, f32[4096,1024]{1,0:T(8,128)} %bitcast.10), custom_call_target="tpu_custom_call" | custom-call | tf_op jit(solution)/shard_map/pallas_call | solution.py:347
  266.0 12.0 %copy.7 = f32[1,4096,1024]{2,1,0:T(8,128)} copy(f32[1,4096,1024]{2,1,0:T(8,128)} %bitcast.9) | data formatting | bytes 33554432
  (1 shorter events, 0.0 us)

commit v2 on v1

--- a/solution.py
+++ b/solution.py
@@ -1,4 +1,5 @@
 import functools
+import math
 
 import jax
 import jax.numpy as jnp
@@ -25,11 +26,15 @@
 
 
 def front_kernel(
-    n, inv_in, up_in, low_in, map_ref, base_in, x_out,
-    up, inv, low, up_h, up_l, inv_h, inv_l, low_h, low_l, lx_h, lx_l, f_buf, f_h, f_l, x_buf,
+    n, limits, inv_in, up_in, low_in, index_ref, base_in, x_out,
+    map_ref, up, inv, low, up_h, up_l, inv_h, inv_l, low_h, low_l, lx_h, lx_l, f_buf, f_h, f_l, x_buf,
     local_sem, part_send, part_recv, up_send, up_recv, inv_send, inv_recv,
-    low_send, low_recv, f_send, f_recv, in_sem, out_sem,
+    low_send, low_recv, f_send, f_recv, in_sem, out_sem, *packing,
 ):
+    packed = limits is not None
+    if packed:
+        ranks, want, row_want, row_in, c_out, c_in, c_h, c_l, g_h, g_l, c_send, c_recv = packing
+        cap, cross = limits
     t = lax.axis_index("tile")
     f = lax.axis_index("front")
     partner = lax.rem(f, 2) * -2 + 1 + f
@@ -43,6 +48,10 @@
     middle = (t >= 1) & (t <= n - 2)
     at_end = (t == 0) | (t == n - 1)
     lower = t < n // 2
+    server = (t == 1) | (t == n - 2)
+    end = lax.div(t - 1, n - 3) * (n - 1)
+    aside = lax.rem(t + 1, n)
+    first = jnp.where(lower, 0, n // 2) if packed else 0
 
     barrier = pltpu.get_barrier_semaphore()
     pl.semaphore_signal(barrier, inc=1, device_id=(partner, t), device_id_type=MESH)
@@ -66,19 +75,22 @@
     sources = (up_in, inv_in, low_in)
     targets = (up, inv, low)
 
+    def place(kind, child, shard):
+        return targets[kind].at[child, shard - first if kind == 0 else shard]
+
     def local(kind):
-        return pltpu.make_async_copy(sources[kind].at[0], targets[kind].at[0, t], local_sem.at[kind])
+        return pltpu.make_async_copy(sources[kind].at[0], place(kind, 0, t), local_sem.at[kind])
 
     def exchange(kind):
         return pltpu.make_async_remote_copy(
-            src_ref=sources[kind].at[1], dst_ref=targets[kind].at[1, t],
+            src_ref=sources[kind].at[1], dst_ref=place(kind, 1, t),
             send_sem=part_send.at[kind], recv_sem=part_recv.at[kind],
             device_id=(partner, t), device_id_type=MESH,
         )
 
     def hop(kind, child, shard, side):
         send, recv = ((up_send, up_recv), (inv_send, inv_recv), (low_send, low_recv))[kind]
-        ref = targets[kind].at[child, shard]
+        ref = place(kind, child, shard)
         return pltpu.make_async_remote_copy(
             src_ref=ref, dst_ref=ref,
             send_sem=send.at[side, child, shard], recv_sem=recv.at[child, shard],
@@ -88,6 +100,8 @@
     def takes(kind, side):
         if kind == 2:
             return t + 1 <= n - 1 if side == 0 else t - 1 >= 0
+        if kind == 0 and packed:
+            return t == 0 if side == 0 else t == n - 1
         return t + 1 <= n - 2 if side == 0 else t - 1 >= 1
 
     def send(kind, child, shard, side):
@@ -113,17 +127,102 @@
         pass_on((2,), child, d, 0, t >= 0)
         pass_on((2,), child, d, 1, t >= 0)
 
+    kinds = (1,) if packed else (1, 0)
+
     def near(child):
         @pl.loop(1, n)
         def _(d):
-            pass_on((1, 0), child, d, 0, middle & lower)
-            pass_on((1, 0), child, d, 1, middle & (t >= n // 2))
+            pass_on(kinds, child, d, 0, middle & lower)
+            pass_on(kinds, child, d, 1, middle & (t >= n // 2))
 
     def far(child):
         @pl.loop(1, n)
         def _(d):
-            pass_on((1, 0), child, d, 1, middle & lower)
-            pass_on((1, 0), child, d, 0, middle & (t >= n // 2))
+            pass_on(kinds, child, d, 1, middle & lower)
+            pass_on(kinds, child, d, 0, middle & (t >= n // 2))
+
+    def listed(child, shard):
+        return map_ref[child, :, pl.ds(pl.multiple_of(shard * wc, wc), wc)]
+
+    def tables(child):
+        row = lax.broadcasted_iota(jnp.int32, (8, 1), 0)
+        half, side = width // 2, order // 2
+        tile = jnp.where(middle, end, t) * width
+        ours = jnp.where(lower, 0, side)
+        starts = (tile, tile + half, side - ours, ours)
+        spans = (half, half, side, side)
+        low_end = high_end = jnp.zeros((8, 1), jnp.int32)
+        for q in range(4):
+            low_end = jnp.where(row == q, starts[q], low_end)
+            high_end = jnp.where(row == q, starts[q] + spans[q], high_end)
+        before = lax.broadcasted_iota(jnp.int32, (wc, wc), 0) < lax.broadcasted_iota(jnp.int32, (wc, wc), 1)
+        before = one_hot(before)
+        passed = jnp.zeros((8, 1), jnp.float32)
+        which = lax.broadcasted_iota(jnp.int32, (8, wc), 0)
+        wants = [jnp.zeros((cap, 8), jnp.float32)] * 2
+        rows = [jnp.zeros((8, row_want.shape[3]), jnp.float32)] * 2
+        inward = jnp.zeros((8, row_in.shape[2]), jnp.float32)
+        for s in range(n):
+            columns = map_ref[child, :, s * wc:(s + 1) * wc]
+            is_ours = (first <= s) & (s < first + n // 2)
+            fits = (row < 2) | ((row == 2) & is_ours) | ((row == 3) & ~is_ours)
+            inside = (columns >= low_end) & (columns < high_end) & fits
+            mark = one_hot(inside)
+            rank = jnp.where(inside, (dot(mark, before) + passed).astype(jnp.int32), -1)
+            passed = passed + jnp.sum(mark.astype(jnp.float32), axis=1, keepdims=True)
+            ranks[child, :, s * wc:(s + 1) * wc] = rank
+            digits = jnp.where(which == 0, columns >> 7, jnp.where(which == 1, columns & 127, 1))
+            digits = digits.astype(jnp.float32).astype(jnp.bfloat16)
+
+            def pick(q, size):
+                return one_hot(lax.broadcasted_iota(jnp.int32, (size, wc), 0) == rank[q:q + 1])
+
+            for h in range(2):
+                wants[h] = wants[h] + dot(pick(h, cap), digits, (1, 1))
+                rows[h] = rows[h] + dot(digits, pick(h, row_want.shape[3]), (1, 1))
+            inward = inward + dot(digits, pick(3, row_in.shape[2]), (1, 1))
+
+        def across(found):
+            value = found[0:1].astype(jnp.int32) * 128 + found[1:2].astype(jnp.int32)
+            return jnp.where(found[2:3] > 0, value, -1)
+
+        for h in range(2):
+            found = wants[h].astype(jnp.int32)
+            want[child, h] = jnp.where(found[:, 2:3] > 0, found[:, 0:1] * 128 + found[:, 1:2], -1)
+            row_want[child, h] = across(rows[h])
+        row_in[child] = across(inward)
+
+    def cross_copy(child):
+        return pltpu.make_async_remote_copy(
+            src_ref=c_out.at[child], dst_ref=c_in.at[child],
+            send_sem=c_send.at[child], recv_sem=c_recv.at[child],
+            device_id=(f, n - 1 - t), device_id_type=MESH,
+        )
+
+    def pack(child):
+        @pl.when(middle)
+        def _():
+            @pl.when(lower)
+            def _():
+                hop(0, child, 0, 0).wait_recv()
+
+            @pl.when(t >= n // 2)
+            def _():
+                hop(0, child, n - 1, 1).wait_recv()
+
+            for k in range(n // 2):
+                high, low_part = parts(up[child, k])
+                up_h[child, k] = high
+                up_l[child, k] = low_part
+            total = None
+            for k in range(n // 2):
+                shard = pl.ds(pl.multiple_of((first + k) * wc, wc), wc)
+                rank = ranks[child, 2:3, shard]
+                choose = one_hot(lax.broadcasted_iota(jnp.int32, (cross, wc), 0) == rank)
+                piece = dot(choose, up_h[child, k], (1, 1)) + dot(choose, up_l[child, k], (1, 1))
+                total = piece if total is None else total + piece
+            c_out[child] = total
+            cross_copy(child).start()
 
     def place_rows(child):
         @pl.loop(0, n)
@@ -144,25 +243,39 @@
             lx_l[child, pl.ds(base, span), :] = dot(choose, low_l[...]).astype(jnp.bfloat16)
 
     def split_child(child):
+        if packed:
+            cross_copy(child).wait_recv()
+            high, low_part = parts(c_in[child])
+            rest = jnp.zeros((c_h.shape[0] - cross, c_h.shape[1]), jnp.bfloat16)
+            c_h[:cross] = high
+            c_l[:cross] = low_part
+            c_h[cross:] = rest
+            c_l[cross:] = rest
+
         @pl.loop(0, n)
         def _(s):
-            high, low_part = parts(up[child, s])
-            up_h[s] = high
-            up_l[s] = low_part
+            if not packed:
+                high, low_part = parts(up[child, s])
+                up_h[s] = high
+                up_l[s] = low_part
             rows = pl.ds(pl.multiple_of(s * kr, kr), kr)
             high, low_part = parts(inv[child, s])
             inv_h[rows, :] = high
             inv_l[rows, :] = low_part
 
-    def factor(child, start, j):
-        columns = lax.broadcasted_iota(jnp.int32, (chunk, wc), 0) + (start + j * chunk)
+    def factor(child, columns):
         high = low_part = None
-        for s in range(n):
-            choose = one_hot(columns == map_ref[child, :, s * wc:(s + 1) * wc])
-            a = dot(choose, up_h[s], (1, 1))
-            b = dot(choose, up_l[s], (1, 1))
+        for s in range(n // 2 if packed else n):
+            choose = one_hot(columns == listed(child, first + s))
+            index = (child, s) if packed else s
+            a = dot(choose, up_h[index], (1, 1))
+            b = dot(choose, up_l[index], (1, 1))
             high = a if high is None else high + a
             low_part = b if low_part is None else low_part + b
+        if packed:
+            choose = one_hot(columns == row_in[child])
+            high = high + dot(choose, c_h[...])
+            low_part = low_part + dot(choose, c_l[...])
         high = high.astype(jnp.bfloat16)
         low_part = low_part.astype(jnp.bfloat16)
         total = dot(high, inv_h[...], (1, 1))
@@ -172,18 +285,19 @@
     def strip(j):
         return pl.ds(pl.multiple_of(j * chunk, chunk), chunk)
 
+    def range_of(start):
+        return lax.broadcasted_iota(jnp.int32, (chunk, 1), 0) + start
+
+    groups = 2 if packed else chunks
+
     def end_copy(child, j, target):
-        ref = f_buf.at[child, strip(j)]
+        ref = f_buf.at[child, j]
         return pltpu.make_async_remote_copy(
             src_ref=ref, dst_ref=ref,
             send_sem=f_send.at[child, j], recv_sem=f_recv.at[child, j],
             device_id=(f, target), device_id_type=MESH,
         )
 
-    server = (t == 1) | (t == n - 2)
-    end = lax.div(t - 1, n - 3) * (n - 1)
-    aside = lax.rem(t + 1, n)
-
     def serve(child):
         @pl.when(middle)
         def _():
@@ -191,24 +305,45 @@
 
             @pl.when(server)
             def _():
-                @pl.loop(0, chunks)
+                @pl.loop(0, groups)
                 def _(j):
-                    f_buf[child, strip(j), :] = factor(child, end * width, j)
+                    columns = want[child, j] if packed else range_of(end * width + j * chunk)
+                    f_buf[child, j] = factor(child, columns)
                     end_copy(child, j, end).start()
 
             @pl.loop(0, chunks)
             def _(j):
-                high, low_part = parts(factor(child, t * width, j))
+                high, low_part = parts(factor(child, range_of(t * width + j * chunk)))
                 f_h[child, strip(j), :] = high
                 f_l[child, strip(j), :] = low_part
 
     def take_factor(child, j):
-        @pl.when(at_end)
+        if packed:
+            fresh = at_end & (lax.rem(j, chunks // 2) == 0)
+            group = lax.div(j, chunks // 2)
+        else:
+            fresh, group = at_end, j
+
+        @pl.when(fresh)
         def _():
-            end_copy(child, j, aside).wait_recv()
-            high, low_part = parts(f_buf[child, strip(j), :])
-            f_h[child, strip(j), :] = high
-            f_l[child, strip(j), :] = low_part
+            end_copy(child, group, aside).wait_recv()
+            high, low_part = parts(f_buf[child, group])
+            if packed:
+                rest = jnp.zeros((g_h.shape[0] - cap, g_h.shape[1]), jnp.bfloat16)
+                g_h[:cap] = high
+                g_l[:cap] = low_part
+                g_h[cap:] = rest
+                g_l[cap:] = rest
+            else:
+                f_h[child, strip(j), :] = high
+                f_l[child, strip(j), :] = low_part
+
+        if packed:
+            @pl.when(at_end)
+            def _():
+                choose = one_hot(range_of(t * width + j * chunk) == row_want[child, group])
+                f_h[child, strip(j), :] = dot(choose, g_h[...]).astype(jnp.bfloat16)
+                f_l[child, strip(j), :] = dot(choose, g_l[...]).astype(jnp.bfloat16)
 
     slots = x_buf.shape[0]
     ahead = slots // 2
@@ -281,21 +416,29 @@
             send_own(1, child)
             send_own(0, child)
 
+    for child in range(2):
+        map_ref[child] = index_ref[f if child == 0 else partner, child:child + 1, :]
+    if packed:
+        for child in range(2):
+            tables(child)
+
     relay_low(0, 1)
     relay_low(1, 1)
 
     @pl.when(middle)
     def _():
-        send_own(1, 0)
-        send_own(0, 0)
+        for kind in kinds:
+            send_own(kind, 0)
 
     relay_low(0, 2)
     near(0)
+    if packed:
+        pack(0)
 
     @pl.when(middle)
     def _():
-        send_own(1, 1)
-        send_own(0, 1)
+        for kind in kinds:
+            send_own(kind, 1)
 
     relay_low(1, 2)
 
@@ -307,6 +450,8 @@
     relay_low(0, n - 1)
     place_rows(0)
     near(1)
+    if packed:
+        pack(1)
     relay_low(1, n - 1)
     place_rows(1)
     far(0)
@@ -327,12 +472,21 @@
 
         @pl.when(server)
         def _():
-            @pl.loop(0, chunks)
+            @pl.loop(0, groups)
             def _(j):
                 end_copy(child, j, aside).wait_send()
 
-
-def assembled(inverse, upper, lower, maps, base, n):
+        if packed:
+            @pl.when(middle)
+            def _():
+                cross_copy(child).wait_send()
+
+
+def capacity(expected):
+    return -(-math.ceil(expected + 2.8 * math.sqrt(expected)) // 16) * 16
+
+
+def assembled(inverse, upper, lower, maps, base, n, limits):
     order, width = base.shape
     pivots = inverse.shape[2]
     count = maps.shape[2]
@@ -343,25 +497,49 @@
     chunk = min(256, width)
     chunks = width // chunk
     slots = 4
+    packed = limits is not None
+    held, extra = n, []
+    f_shape = (2, chunks, chunk, pivots)
+    u_shape = (n, pivots, wc)
+    if packed:
+        cap, cross = limits
+        cap_pad, cross_pad = -(-cap // 128) * 128, -(-cross // 128) * 128
+        held = n // 2
+        f_shape = (2, 2, cap, pivots)
+        u_shape = (2, held, pivots, wc)
+        extra = [
+            vmem((2, 8, count), jnp.int32),
+            vmem((2, 2, cap, 1), jnp.int32),
+            vmem((2, 2, 1, cap_pad), jnp.int32),
+            vmem((2, 1, cross_pad), jnp.int32),
+            vmem((2, cross, pivots), f32),
+            vmem((2, cross, pivots), f32),
+            vmem((cross_pad, pivots), b16),
+            vmem((cross_pad, pivots), b16),
+            vmem((cap_pad, pivots), b16),
+            vmem((cap_pad, pivots), b16),
+            dma((2,)), dma((2,)),
+        ]
     whole = pl.BlockSpec(memory_space=pl.ANY)
     return pl.pallas_call(
-        functools.partial(front_kernel, n),
+        functools.partial(front_kernel, n, limits),
         out_shape=jax.ShapeDtypeStruct((order, width), f32),
         in_specs=[whole] * 3 + [pl.BlockSpec(memory_space=vmem), whole],
         out_specs=whole,
         scratch_shapes=[
-            vmem((2, n, pivots, wc), f32),
+            vmem((2, 1, count), jnp.int32),
+            vmem((2, held, pivots, wc), f32),
             vmem((2, n, kr, pivots), f32),
             vmem((2, n, lr, pivots), f32),
-            vmem((n, pivots, wc), b16),
-            vmem((n, pivots, wc), b16),
+            vmem(u_shape, b16),
+            vmem(u_shape, b16),
             vmem((n * kr, pivots), b16),
             vmem((n * kr, pivots), b16),
             vmem((count, pivots), b16),
             vmem((count, pivots), b16),
             vmem((2, order, pivots), b16),
             vmem((2, order, pivots), b16),
-            vmem((2, width, pivots), f32),
+            vmem(f_shape, f32),
             vmem((2, width, pivots), b16),
             vmem((2, width, pivots), b16),
             vmem((slots, min(1024, order), chunk), f32),
@@ -369,25 +547,39 @@
             dma((2, 2, n)), dma((2, n)),
             dma((2, 2, n)), dma((2, n)),
             dma((2, 2, n)), dma((2, n)),
-            dma((2, chunks)), dma((2, chunks)),
+            dma(f_shape[:2]), dma(f_shape[:2]),
             dma((slots,)), dma((slots,)),
-        ],
+        ] + extra,
         compiler_params=pltpu.CompilerParams(
-            collective_id=0, has_side_effects=True, vmem_limit_bytes=63 * 1024 * 1024
+            collective_id=int(packed), has_side_effects=True, vmem_limit_bytes=63 * 1024 * 1024
         ),
     )(inverse, upper, lower, maps, base)
 
 
 def shards(pivot_inverse, panel_upper, panel_lower, index_map, parent_base):
     n = lax.axis_size("tile")
-    group = lax.axis_index("front")
-    partner = jnp.bitwise_xor(group, 1)
-    maps = jnp.stack([
-        lax.dynamic_index_in_dim(index_map, group, 0, keepdims=False)[0],
-        lax.dynamic_index_in_dim(index_map, partner, 0, keepdims=False)[1],
-    ])
-    return assembled(
-        pivot_inverse[0], panel_upper[0], panel_lower[0], maps[:, None, :], parent_base[0], n
+    order, width = parent_base.shape[1:]
+    count = index_map.shape[2]
+    operands = (pivot_inverse[0], panel_upper[0], panel_lower[0], index_map, parent_base[0])
+
+    def run(limits, *args):
+        return assembled(*args, n, limits)
+
+    half, side = width // 2, order // 2
+    cap = capacity(half * count // order)
+    cross = capacity(count // 4)
+    if n != 4 or cap >= half or cross >= count // 2:
+        return run(None, *operands)[None]
+
+    near = lax.broadcasted_iota(jnp.int32, index_map.shape, 2) < count // 2
+    crossing = near ^ (index_map < side)
+    most = [jnp.max(jnp.sum((crossing & (near ^ flip)).astype(jnp.int32), axis=2)) for flip in (False, True)]
+    fits = jnp.maximum(*most) <= cross
+    for part in (0, 1, 2 * n - 2, 2 * n - 1):
+        inside = (index_map >= part * half) & (index_map < (part + 1) * half)
+        fits &= jnp.max(jnp.sum(inside.astype(jnp.int32), axis=2)) <= cap
+    return lax.cond(
+        fits, functools.partial(run, (cap, cross)), functools.partial(run, None), *operands
     )[None]
 
 

time: 278 us -> 234 us (0.84)
  Pallas kernels: 265 us -> 212 us
  other arithmetic: 0.02 us -> 5.72 us
  between operations: 0.02 us -> 3.99 us
    pallas_call x1, Pallas kernels: 265 us -> 212 us  [assembled(): pl.pallas_call(functools.partial(front_kernel, n, limits), out_shape=jax....]
    reduce_max x0 -> x6, other arithmetic: none -> 3.88 us  [the longest x4 2.54 us: shards(): fits &= jnp.max(jnp.sum(inside.astype(jnp.int32), axis=2)) <= cap]
where the time goes in v2:
time: 234 us
  Pallas kernels  212 us (91%)
  local copies, waits for them, and re-layouts  12 us (5%)
  other arithmetic  5.72 us (2%)
  between operations  3.99 us (2%)
    pallas_call x1, Pallas kernels, assembled(): pl.pallas_call(functools.partial(front_kernel, n, limits), out_shape=jax....  212 us
    unnamed x1, local copies, waits for them, and re-layouts  12 us

profile of v2, /device:TPU:0, one launch (start us, length us, event | category | flops | bytes accessed | tf_op | source)
XLA Modules:
  0.0 234.2 jit_solution(6196646158483972378)
XLA Ops:
  0.0 1.8 fusion.1
  1.8 0.6 reduce_max.59
  3.1 0.6 reduce_max.58
  4.4 0.6 reduce_max.56
  5.7 0.6 reduce_max.57
  7.0 0.6 reduce_max.54
  7.6 0.7 reduce_max.55
  9.7 212.6 %conditional.1 = (f32[1,4096,1024]{2,1,0:T(8,128)}) conditional(s32[]{:T(128)} %convert_element_type.27, (f32[2,128,512]{2,1,0:T(8,128)}, f32[2,512,512]{2,1,0:T(8,128)}, f32[2,512,512]{2,1,0:T(8,128)}, s32[8,2,2048]{2,1,0:T(2,128)}, f32[4096,1024]{1,0:T(8,128)}) %tuple.32, (f32[2,128,512]{2,1,0:T(8,128)}, f32[2,512,512]{2,1,0:T(8,128)}, ...), branch_computations={%region_12.0_spmd, %region_13.0_spmd} | conditional | bytes 8 | solution.py:581
  9.7 212.3 %branch_1_fun.1 = f32[4096,1024]{1,0:T(8,128)} custom-call(f32[2,128,512]{2,1,0:T(8,128)} %get-tuple-element.34.inv_in, f32[2,512,512]{2,1,0:T(8,128)} %get-tuple-element.35.up_in, f32[2,512,512]{2,1,0:T(8,128)} %get-tuple-element.36.low_in, s32[8,2,2048]{2,1,0:T(2,128)} %get-tuple-element.37.index_ref, f32[4096,1024]{1,0:T(8,128)} %get-tuple-element.38.base_in), custom_call_target="tpu_custom_call" | custom-call | tf_op jit(solution)/shard_map/cond/branch_1_fun/pallas_call | solution.py:524
  222.3 12.0 %copy.23 = f32[1,4096,1024]{2,1,0:T(8,128)} copy(f32[1,4096,1024]{2,1,0:T(8,128)} %get-tuple-element.39) | data formatting | bytes 33554432
  (2 shorter events, 0.0 us)

commit v3 on v2

--- a/solution.py
+++ b/solution.py
@@ -26,15 +26,17 @@
 
 
 def front_kernel(
-    n, limits, inv_in, up_in, low_in, index_ref, base_in, x_out,
+    n, limits, inv_in, up_in, low_in, index_ref, base_in,
+    x_out, high_out, low_out, last_h, last_l,
     map_ref, up, inv, low, up_h, up_l, inv_h, inv_l, low_h, low_l, lx_h, lx_l, f_buf, f_h, f_l, x_buf,
     local_sem, part_send, part_recv, up_send, up_recv, inv_send, inv_recv,
-    low_send, low_recv, f_send, f_recv, in_sem, out_sem, *packing,
+    low_send, low_recv, f_send, f_recv, in_sem, out_sem, lx_sem, *packing,
 ):
     packed = limits is not None
     if packed:
         ranks, want, row_want, row_in, c_out, c_in, c_h, c_l, g_h, g_l, c_send, c_recv = packing
         cap, cross = limits
+        gap = -(-cap // 16) * 16
     t = lax.axis_index("tile")
     f = lax.axis_index("front")
     partner = lax.rem(f, 2) * -2 + 1 + f
@@ -146,11 +148,11 @@
 
     def tables(child):
         row = lax.broadcasted_iota(jnp.int32, (8, 1), 0)
-        half, side = width // 2, order // 2
+        side = order // 2
         tile = jnp.where(middle, end, t) * width
         ours = jnp.where(lower, 0, side)
-        starts = (tile, tile + half, side - ours, ours)
-        spans = (half, half, side, side)
+        starts = (tile, tile, side - ours, ours)
+        spans = (width, width, side, side)
         low_end = high_end = jnp.zeros((8, 1), jnp.int32)
         for q in range(4):
             low_end = jnp.where(row == q, starts[q], low_end)
@@ -160,36 +162,36 @@
         passed = jnp.zeros((8, 1), jnp.float32)
         which = lax.broadcasted_iota(jnp.int32, (8, wc), 0)
         wants = [jnp.zeros((cap, 8), jnp.float32)] * 2
-        rows = [jnp.zeros((8, row_want.shape[3]), jnp.float32)] * 2
+        both = jnp.zeros((8, row_want.shape[2]), jnp.float32)
         inward = jnp.zeros((8, row_in.shape[2]), jnp.float32)
         for s in range(n):
             columns = map_ref[child, :, s * wc:(s + 1) * wc]
             is_ours = (first <= s) & (s < first + n // 2)
-            fits = (row < 2) | ((row == 2) & is_ours) | ((row == 3) & ~is_ours)
+            fits = jnp.where(lax.rem(row, 2) == 0, is_ours.astype(jnp.int32), 1 - is_ours.astype(jnp.int32)) > 0
             inside = (columns >= low_end) & (columns < high_end) & fits
             mark = one_hot(inside)
-            rank = jnp.where(inside, (dot(mark, before) + passed).astype(jnp.int32), -1)
+            rank = jnp.where(inside, (dot(mark, before) + passed).astype(jnp.int32), -2 * count)
             passed = passed + jnp.sum(mark.astype(jnp.float32), axis=1, keepdims=True)
             ranks[child, :, s * wc:(s + 1) * wc] = rank
             digits = jnp.where(which == 0, columns >> 7, jnp.where(which == 1, columns & 127, 1))
             digits = digits.astype(jnp.float32).astype(jnp.bfloat16)
 
-            def pick(q, size):
-                return one_hot(lax.broadcasted_iota(jnp.int32, (size, wc), 0) == rank[q:q + 1])
-
-            for h in range(2):
-                wants[h] = wants[h] + dot(pick(h, cap), digits, (1, 1))
-                rows[h] = rows[h] + dot(digits, pick(h, row_want.shape[3]), (1, 1))
-            inward = inward + dot(digits, pick(3, row_in.shape[2]), (1, 1))
+            def pick(q, size, skip=0):
+                return one_hot(lax.broadcasted_iota(jnp.int32, (size, wc), 0) - skip == rank[q:q + 1])
+
+            for q in range(2):
+                wants[q] = wants[q] + dot(pick(q, cap), digits, (1, 1))
+                both = both + dot(digits, pick(q, both.shape[1], q * gap), (1, 1))
+            inward = inward + dot(digits, pick(3, inward.shape[1]), (1, 1))
 
         def across(found):
             value = found[0:1].astype(jnp.int32) * 128 + found[1:2].astype(jnp.int32)
             return jnp.where(found[2:3] > 0, value, -1)
 
-        for h in range(2):
-            found = wants[h].astype(jnp.int32)
-            want[child, h] = jnp.where(found[:, 2:3] > 0, found[:, 0:1] * 128 + found[:, 1:2], -1)
-            row_want[child, h] = across(rows[h])
+        for q in range(2):
+            found = wants[q].astype(jnp.int32)
+            want[child, q] = jnp.where(found[:, 2:3] > 0, found[:, 0:1] * 128 + found[:, 1:2], -1)
+        row_want[child] = across(both)
         row_in[child] = across(inward)
 
     def cross_copy(child):
@@ -232,7 +234,7 @@
             low_h[rows, :] = high
             low_l[rows, :] = low_part
 
-        span = min(256, order)
+        span = min(512, order)
 
         @pl.loop(0, order // span)
         def _(j):
@@ -242,8 +244,67 @@
             lx_h[child, pl.ds(base, span), :] = dot(choose, low_h[...]).astype(jnp.bfloat16)
             lx_l[child, pl.ds(base, span), :] = dot(choose, low_l[...]).astype(jnp.bfloat16)
 
-    def split_child(child):
-        if packed:
+    def split_inverse(child):
+        @pl.loop(0, n)
+        def _(s):
+            rows = pl.ds(pl.multiple_of(s * kr, kr), kr)
+            high, low_part = parts(inv[child, s])
+            inv_h[rows, :] = high
+            inv_l[rows, :] = low_part
+
+    def factor(child, columns, near_side=True, far_side=True):
+        terms = []
+        if near_side:
+            for s in range(n // 2 if packed else n):
+                choose = one_hot(columns == listed(child, first + s))
+                index = (child, s) if packed else s
+                terms.append((dot(choose, up_h[index], (1, 1)), dot(choose, up_l[index], (1, 1))))
+        if packed and far_side:
+            choose = one_hot(columns == row_in[child])
+            terms.append((dot(choose, c_h[...]), dot(choose, c_l[...])))
+        high, low_part = terms[0]
+        for a, b in terms[1:]:
+            high = high + a
+            low_part = low_part + b
+        high = high.astype(jnp.bfloat16)
+        low_part = low_part.astype(jnp.bfloat16)
+        total = dot(high, inv_h[...], (1, 1))
+        total = total + dot(low_part, inv_h[...], (1, 1))
+        return total + dot(high, inv_l[...], (1, 1))
+
+    def strip(j):
+        return pl.ds(pl.multiple_of(j * chunk, chunk), chunk)
+
+    def range_of(start):
+        return lax.broadcasted_iota(jnp.int32, (chunk, 1), 0) + start
+
+    groups = 2 if packed else chunks
+
+    def end_copy(child, j, target):
+        ref = f_buf.at[child, j]
+        return pltpu.make_async_remote_copy(
+            src_ref=ref, dst_ref=ref,
+            send_sem=f_send.at[child, j], recv_sem=f_recv.at[child, j],
+            device_id=(f, target), device_id_type=MESH,
+        )
+
+    def kept(child):
+        return (f_h, f_l) if child == 0 else (last_h, last_l)
+
+    def keep(child, j, value):
+        for ref, part in zip(kept(child), parts(value)):
+            ref[strip(j), :] = part
+
+    def serve_near(child):
+        @pl.when(middle)
+        def _():
+            split_inverse(child)
+            f_buf[child, 0] = factor(child, want[child, 0], far_side=False)
+            end_copy(child, 0, end).start()
+
+    def serve_far(child):
+        @pl.when(middle)
+        def _():
             cross_copy(child).wait_recv()
             high, low_part = parts(c_in[child])
             rest = jnp.zeros((c_h.shape[0] - cross, c_h.shape[1]), jnp.bfloat16)
@@ -251,99 +312,56 @@
             c_l[:cross] = low_part
             c_h[cross:] = rest
             c_l[cross:] = rest
-
-        @pl.loop(0, n)
-        def _(s):
-            if not packed:
+            f_buf[child, 1] = factor(child, want[child, 1], near_side=False)
+            end_copy(child, 1, end).start()
+
+    def serve_all(child):
+        @pl.when(middle)
+        def _():
+            split_inverse(child)
+
+            @pl.loop(0, n)
+            def _(s):
                 high, low_part = parts(up[child, s])
                 up_h[s] = high
                 up_l[s] = low_part
-            rows = pl.ds(pl.multiple_of(s * kr, kr), kr)
-            high, low_part = parts(inv[child, s])
-            inv_h[rows, :] = high
-            inv_l[rows, :] = low_part
-
-    def factor(child, columns):
-        high = low_part = None
-        for s in range(n // 2 if packed else n):
-            choose = one_hot(columns == listed(child, first + s))
-            index = (child, s) if packed else s
-            a = dot(choose, up_h[index], (1, 1))
-            b = dot(choose, up_l[index], (1, 1))
-            high = a if high is None else high + a
-            low_part = b if low_part is None else low_part + b
-        if packed:
-            choose = one_hot(columns == row_in[child])
-            high = high + dot(choose, c_h[...])
-            low_part = low_part + dot(choose, c_l[...])
-        high = high.astype(jnp.bfloat16)
-        low_part = low_part.astype(jnp.bfloat16)
-        total = dot(high, inv_h[...], (1, 1))
-        total = total + dot(low_part, inv_h[...], (1, 1))
-        return total + dot(high, inv_l[...], (1, 1))
-
-    def strip(j):
-        return pl.ds(pl.multiple_of(j * chunk, chunk), chunk)
-
-    def range_of(start):
-        return lax.broadcasted_iota(jnp.int32, (chunk, 1), 0) + start
-
-    groups = 2 if packed else chunks
-
-    def end_copy(child, j, target):
-        ref = f_buf.at[child, j]
-        return pltpu.make_async_remote_copy(
-            src_ref=ref, dst_ref=ref,
-            send_sem=f_send.at[child, j], recv_sem=f_recv.at[child, j],
-            device_id=(f, target), device_id_type=MESH,
-        )
-
-    def serve(child):
-        @pl.when(middle)
-        def _():
-            split_child(child)
 
             @pl.when(server)
             def _():
-                @pl.loop(0, groups)
+                @pl.loop(0, chunks)
                 def _(j):
-                    columns = want[child, j] if packed else range_of(end * width + j * chunk)
-                    f_buf[child, j] = factor(child, columns)
+                    f_buf[child, j] = factor(child, range_of(end * width + j * chunk))
                     end_copy(child, j, end).start()
 
+    def serve_own(child):
+        @pl.when(middle)
+        def _():
             @pl.loop(0, chunks)
             def _(j):
-                high, low_part = parts(factor(child, range_of(t * width + j * chunk)))
-                f_h[child, strip(j), :] = high
-                f_l[child, strip(j), :] = low_part
-
-    def take_factor(child, j):
-        if packed:
-            fresh = at_end & (lax.rem(j, chunks // 2) == 0)
-            group = lax.div(j, chunks // 2)
-        else:
-            fresh, group = at_end, j
-
-        @pl.when(fresh)
-        def _():
-            end_copy(child, group, aside).wait_recv()
-            high, low_part = parts(f_buf[child, group])
+                keep(child, j, factor(child, range_of(t * width + j * chunk)))
+
+    def take_factor(child):
+        @pl.when(at_end)
+        def _():
             if packed:
-                rest = jnp.zeros((g_h.shape[0] - cap, g_h.shape[1]), jnp.bfloat16)
-                g_h[:cap] = high
-                g_l[:cap] = low_part
-                g_h[cap:] = rest
-                g_l[cap:] = rest
-            else:
-                f_h[child, strip(j), :] = high
-                f_l[child, strip(j), :] = low_part
-
-        if packed:
-            @pl.when(at_end)
-            def _():
-                choose = one_hot(range_of(t * width + j * chunk) == row_want[child, group])
-                f_h[child, strip(j), :] = dot(choose, g_h[...]).astype(jnp.bfloat16)
-                f_l[child, strip(j), :] = dot(choose, g_l[...]).astype(jnp.bfloat16)
+                for q in range(2):
+                    end_copy(child, q, aside).wait_recv()
+                    high, low_part = parts(f_buf[child, q])
+                    for ref, part in ((g_h, high), (g_l, low_part)):
+                        ref[q * gap:q * gap + cap] = part
+                        stop = gap if q == 0 else ref.shape[0]
+                        if q * gap + cap < stop:
+                            ref[q * gap + cap:stop] = jnp.zeros((stop - q * gap - cap, ref.shape[1]), jnp.bfloat16)
+
+            @pl.loop(0, chunks)
+            def _(j):
+                if packed:
+                    choose = one_hot(range_of(t * width + j * chunk) == row_want[child])
+                    for ref, source in zip(kept(child), (g_h, g_l)):
+                        ref[strip(j), :] = dot(choose, source[...]).astype(jnp.bfloat16)
+                else:
+                    end_copy(child, j, aside).wait_recv()
+                    keep(child, j, f_buf[child, j])
 
     slots = x_buf.shape[0]
     ahead = slots // 2
@@ -355,12 +373,10 @@
         rows = pl.ds(pl.multiple_of(lax.rem(i, per) * tall, tall), tall)
         return ref.at[rows, strip(lax.div(i, per))]
 
-    def subtract(child):
-        source = base_in if child == 0 else x_out
-
+    def subtract():
         def load(i):
             slot = lax.rem(i, slots)
-            return pltpu.make_async_copy(window(source, i), x_buf.at[slot], in_sem.at[slot])
+            return pltpu.make_async_copy(window(base_in, i), x_buf.at[slot], in_sem.at[slot])
 
         def store(i):
             slot = lax.rem(i, slots)
@@ -368,14 +384,11 @@
 
         for i in range(ahead):
             load(i).start()
+        take_factor(0)
 
         @pl.loop(0, blocks)
         def _(i):
             j = lax.div(i, per)
-
-            @pl.when(lax.rem(i, per) == 0)
-            def _():
-                take_factor(child, j)
 
             @pl.when(i + ahead < blocks)
             def _():
@@ -386,11 +399,11 @@
                 load(i + ahead).start()
 
             rows = pl.ds(pl.multiple_of(lax.rem(i, per) * tall, tall), tall)
-            high = f_h[child, strip(j), :]
-            left = lx_h[child, rows, :]
+            high = f_h[strip(j), :]
+            left = lx_h[0, rows, :]
             total = dot(left, high, (1, 1))
-            total = total + dot(left, f_l[child, strip(j), :], (1, 1))
-            total = total + dot(lx_l[child, rows, :], high, (1, 1))
+            total = total + dot(left, f_l[strip(j), :], (1, 1))
+            total = total + dot(lx_l[0, rows, :], high, (1, 1))
             load(i).wait()
             slot = lax.rem(i, slots)
             x_buf[slot] = x_buf[slot] - total
@@ -398,6 +411,9 @@
 
         for i in range(max(blocks - slots, 0), blocks):
             store(i).wait()
+
+    def hand_on(k):
+        return pltpu.make_async_copy((lx_h, lx_l)[k].at[1], (high_out, low_out)[k], lx_sem.at[k])
 
     for kind in (2, 1, 0):
         exchange(kind).start()
@@ -412,9 +428,8 @@
 
     @pl.when(at_end)
     def _():
-        for child in range(2):
-            send_own(1, child)
-            send_own(0, child)
+        for kind, child in ((1, 0), (1, 1), (0, 0), (0, 1)) if packed else ((1, 0), (0, 0), (1, 1), (0, 1)):
+            send_own(kind, child)
 
     for child in range(2):
         map_ref[child] = index_ref[f if child == 0 else partner, child:child + 1, :]
@@ -427,18 +442,22 @@
 
     @pl.when(middle)
     def _():
-        for kind in kinds:
-            send_own(kind, 0)
-
-    relay_low(0, 2)
-    near(0)
+        for kind, child in ((1, 0), (1, 1)) if packed else ((1, 0), (0, 0)):
+            send_own(kind, child)
+
     if packed:
+        near(0)
+        near(1)
+        relay_low(0, 2)
         pack(0)
-
-    @pl.when(middle)
-    def _():
-        for kind in kinds:
-            send_own(kind, 1)
+    else:
+        relay_low(0, 2)
+        near(0)
+
+        @pl.when(middle)
+        def _():
+            send_own(1, 1)
+            send_own(0, 1)
 
     relay_low(1, 2)
 
@@ -449,17 +468,33 @@
 
     relay_low(0, n - 1)
     place_rows(0)
-    near(1)
     if packed:
         pack(1)
+    else:
+        near(1)
     relay_low(1, n - 1)
     place_rows(1)
+    for k in range(2):
+        hand_on(k).start()
     far(0)
-    serve(0)
-    subtract(0)
-    far(1)
-    serve(1)
-    subtract(1)
+    if packed:
+        serve_near(0)
+        serve_far(0)
+        serve_own(0)
+        far(1)
+        serve_near(1)
+        subtract()
+        serve_far(1)
+    else:
+        serve_all(0)
+        serve_own(0)
+        subtract()
+        far(1)
+        serve_all(1)
+    serve_own(1)
+    take_factor(1)
+    for k in range(2):
+        hand_on(k).wait()
 
     for child in range(2):
         @pl.loop(0, n)
@@ -482,8 +517,9 @@
                 cross_copy(child).wait_send()
 
 
-def capacity(expected):
-    return -(-math.ceil(expected + 2.8 * math.sqrt(expected)) // 16) * 16
+def capacity(draws, share):
+    spread = math.sqrt(draws * share * (1 - share))
+    return -(-math.ceil(draws * share + 4 * spread) // 8) * 8
 
 
 def assembled(inverse, upper, lower, maps, base, n, limits):
@@ -503,14 +539,15 @@
     u_shape = (n, pivots, wc)
     if packed:
         cap, cross = limits
-        cap_pad, cross_pad = -(-cap // 128) * 128, -(-cross // 128) * 128
+        cap_pad = -(-(-(-cap // 16) * 16 + cap) // 128) * 128
+        cross_pad = -(-cross // 128) * 128
         held = n // 2
         f_shape = (2, 2, cap, pivots)
         u_shape = (2, held, pivots, wc)
         extra = [
             vmem((2, 8, count), jnp.int32),
             vmem((2, 2, cap, 1), jnp.int32),
-            vmem((2, 2, 1, cap_pad), jnp.int32),
+            vmem((2, 1, cap_pad), jnp.int32),
             vmem((2, 1, cross_pad), jnp.int32),
             vmem((2, cross, pivots), f32),
             vmem((2, cross, pivots), f32),
@@ -523,9 +560,11 @@
     whole = pl.BlockSpec(memory_space=pl.ANY)
     return pl.pallas_call(
         functools.partial(front_kernel, n, limits),
-        out_shape=jax.ShapeDtypeStruct((order, width), f32),
+        out_shape=[jax.ShapeDtypeStruct((order, width), f32)]
+        + [jax.ShapeDtypeStruct((order, pivots), b16)] * 2
+        + [jax.ShapeDtypeStruct((width, pivots), b16)] * 2,
         in_specs=[whole] * 3 + [pl.BlockSpec(memory_space=vmem), whole],
-        out_specs=whole,
+        out_specs=[whole] * 3 + [pl.BlockSpec(memory_space=vmem)] * 2,
         scratch_shapes=[
             vmem((2, 1, count), jnp.int32),
             vmem((2, held, pivots, wc), f32),
@@ -540,15 +579,15 @@
             vmem((2, order, pivots), b16),
             vmem((2, order, pivots), b16),
             vmem(f_shape, f32),
-            vmem((2, width, pivots), b16),
-            vmem((2, width, pivots), b16),
+            vmem((width, pivots), b16),
+            vmem((width, pivots), b16),
             vmem((slots, min(1024, order), chunk), f32),
             dma((3,)), dma((3,)), dma((3,)),
             dma((2, 2, n)), dma((2, n)),
             dma((2, 2, n)), dma((2, n)),
             dma((2, 2, n)), dma((2, n)),
             dma(f_shape[:2]), dma(f_shape[:2]),
-            dma((slots,)), dma((slots,)),
+            dma((slots,)), dma((slots,)), dma((2,)),
         ] + extra,
         compiler_params=pltpu.CompilerParams(
             collective_id=int(packed), has_side_effects=True, vmem_limit_bytes=63 * 1024 * 1024
@@ -556,6 +595,44 @@
     )(inverse, upper, lower, maps, base)
 
 
+def finish_kernel(x_ref, high_ref, low_ref, f_h, f_l, out_ref):
+    width = out_ref.shape[1]
+    chunk = min(256, width)
+    for j in range(width // chunk):
+        columns = slice(j * chunk, (j + 1) * chunk)
+        total = dot(high_ref[...], f_h[columns, :], (1, 1))
+        total = total + dot(high_ref[...], f_l[columns, :], (1, 1))
+        total = total + dot(low_ref[...], f_h[columns, :], (1, 1))
+        out_ref[:, columns] = x_ref[:, columns] - total
+
+
+def finished(x, high, low_part, f_h, f_l):
+    order, width = x.shape
+    rows = min(1024, order)
+    tall = pl.BlockSpec((rows, width), lambda i: (i, 0))
+    slim = pl.BlockSpec((rows, high.shape[1]), lambda i: (i, 0))
+    fixed = pl.BlockSpec(f_h.shape, lambda i: (0, 0))
+    return pl.pallas_call(
+        finish_kernel,
+        out_shape=jax.ShapeDtypeStruct(x.shape, x.dtype),
+        grid=(order // rows,),
+        in_specs=[tall, slim, slim, fixed, fixed],
+        out_specs=tall,
+        compiler_params=pltpu.CompilerParams(vmem_limit_bytes=40 * 1024 * 1024),
+    )(x, high, low_part, f_h, f_l)
+
+
+def fits_kernel(ranges, index_ref, out_ref):
+    index = index_ref[...]
+    early = lax.broadcasted_iota(jnp.int32, index.shape, 2) < index.shape[2] // 2
+    over = None
+    for start, stop, is_early, limit in ranges:
+        inside = (index >= start) & (index < stop) & (early if is_early else ~early)
+        extra = jnp.sum(inside.astype(jnp.int32), axis=2, keepdims=True) - limit
+        over = extra if over is None else jnp.maximum(over, extra)
+    out_ref[0] = (jnp.max(over) <= 0).astype(jnp.int32)
+
+
 def shards(pivot_inverse, panel_upper, panel_lower, index_map, parent_base):
     n = lax.axis_size("tile")
     order, width = parent_base.shape[1:]
@@ -563,24 +640,28 @@
     operands = (pivot_inverse[0], panel_upper[0], panel_lower[0], index_map, parent_base[0])
 
     def run(limits, *args):
-        return assembled(*args, n, limits)
-
-    half, side = width // 2, order // 2
-    cap = capacity(half * count // order)
-    cross = capacity(count // 4)
-    if n != 4 or cap >= half or cross >= count // 2:
-        return run(None, *operands)[None]
-
-    near = lax.broadcasted_iota(jnp.int32, index_map.shape, 2) < count // 2
-    crossing = near ^ (index_map < side)
-    most = [jnp.max(jnp.sum((crossing & (near ^ flip)).astype(jnp.int32), axis=2)) for flip in (False, True)]
-    fits = jnp.maximum(*most) <= cross
-    for part in (0, 1, 2 * n - 2, 2 * n - 1):
-        inside = (index_map >= part * half) & (index_map < (part + 1) * half)
-        fits &= jnp.max(jnp.sum(inside.astype(jnp.int32), axis=2)) <= cap
-    return lax.cond(
-        fits, functools.partial(run, (cap, cross)), functools.partial(run, None), *operands
-    )[None]
+        return tuple(assembled(*args, n, limits))
+
+    side = order // 2
+    cap = capacity(count // 2, width / order)
+    cross = capacity(count // 2, 1 / 2)
+    if n != 4 or 2 * cap >= width or cross >= count // 2:
+        return finished(*run(None, *operands))[None]
+
+    ranges = (
+        (side, order, True, cross), (0, side, False, cross),
+        (0, width, True, cap), (0, width, False, cap),
+        (order - width, order, True, cap), (order - width, order, False, cap),
+    )
+    fits = pl.pallas_call(
+        functools.partial(fits_kernel, ranges),
+        out_shape=jax.ShapeDtypeStruct((1,), jnp.int32),
+        in_specs=[pl.BlockSpec(memory_space=pltpu.VMEM)],
+        out_specs=pl.BlockSpec(memory_space=pltpu.SMEM),
+    )(index_map)[0]
+    return finished(*lax.cond(
+        fits > 0, functools.partial(run, (cap, cross)), functools.partial(run, None), *operands
+    ))[None]
 
 
 def solution(mesh):

time: 234 us -> 225 us (0.962)
  Pallas kernels: 212 us -> 224 us
  local copies, waits for them, and re-layouts: 12 us -> 0 us
  other arithmetic: 5.72 us -> 0 us
  between operations: 3.99 us -> 0.67 us
    unnamed x1 -> x0, local copies, waits for them, and re-layouts: 12 us -> none
    pallas_call x1 -> x3, Pallas kernels: 212 us -> 224 us  [the longest x1 202 us: assembled(): pl.pallas_call(functools.partial(front_kernel, n, limits), out_shape=[jax...]
    reduce_max x6 -> x0, other arithmetic: 3.88 us -> none  [the longest x4 2.54 us: shards(): fits &= jnp.max(jnp.sum(inside.astype(jnp.int32), axis=2)) <= cap]
where the time goes in v3:
time: 225 us
  Pallas kernels  224 us (100%)
    pallas_call x1, Pallas kernels, assembled(): pl.pallas_call(functools.partial(front_kernel, n, limits), out_shape=[jax...  202 us
    pallas_call x1, Pallas kernels, finished(): pl.pallas_call(finish_kernel, out_shape=jax.ShapeDtypeStruct(x.shape, x.d...  20.5 us

profile of v3, /device:TPU:0, one launch (start us, length us, event | category | flops | bytes accessed | tf_op | source)
XLA Modules:
  0.0 225.1 jit_solution(12581954776428156517)
XLA Ops:
  0.0 2.0 shard_map.55
  2.7 201.9 %conditional.1 = ((f32[4096,1024]{1,0:T(8,128)}, bf16[4096,512]{1,0:T(8,128)(2,1)}, bf16[4096,512]{1,0:T(8,128)(2,1)}, bf16[1024,512]{1,0:T(8,128)(2,1)}, bf16[1024,512]{1,0:T(8,128)(2,1)})) conditional(s32[]{:T(128)} %bitcast, (f32[2,128,512]{2,1,0:T(8,128)}, f32[2,512,512]{2,1,0:T(8,128)}, f32[2,512,512]{2,1,0:T(8,128)}, s32[8,2,2048]{2,1,0:T(2,128)}, ...), branch_computations={%region_0.0_spmd, %region_1.0_spmd} | conditional | bytes 8 | solution.py:662
  2.7 201.6 %branch_1_fun.1 = (f32[4096,1024]{1,0:T(8,128)}, bf16[4096,512]{1,0:T(8,128)(2,1)}, bf16[4096,512]{1,0:T(8,128)(2,1)}, bf16[1024,512]{1,0:T(8,128)(2,1)}, bf16[1024,512]{1,0:T(8,128)(2,1)}) custom-call(f32[2,128,512]{2,1,0:T(8,128)} %get-tuple-element.30.inv_in, f32[2,512,512]{2,1,0:T(8,128)} %get-tuple-element.31.up_in, ...), custom_call_target="tpu_custom_call" | custom-call | tf_op jit(solution)/shard_map/cond/branch_1_fun/pallas_call | solution.py:561
  204.6 20.5 %shard_map.56 = f32[4096,1024]{1,0:T(8,128)} custom-call(f32[4096,1024]{1,0:T(8,128)} %get-tuple-element.40.x_ref, bf16[4096,512]{1,0:T(8,128)(2,1)} %get-tuple-element.41.high_ref, bf16[4096,512]{1,0:T(8,128)(2,1)} %get-tuple-element.42.low_ref, bf16[1024,512]{1,0:T(8,128)(2,1)} %get-tuple-element.43.f_h, bf16[1024,512]{1,0:T(8,128)(2,1)} %get-tuple-element.44.f_l), custom_call_target="tpu_custom_call" | custom-call | tf_op jit(solution)/shard_map/pallas_call | solution.py:615

commit v4 on v3

--- a/solution.py
+++ b/solution.py
@@ -16,6 +16,14 @@
     return high, (value - high.astype(jnp.float32)).astype(jnp.bfloat16)
 
 
+def spread(value, targets):
+    rows = value.shape[0]
+    for ref, part in zip(targets, parts(value)):
+        ref[:rows] = part
+        if rows < ref.shape[0]:
+            ref[rows:] = jnp.zeros((ref.shape[0] - rows, ref.shape[1]), jnp.bfloat16)
+
+
 def dot(left, right, contract=(1, 0)):
     dims = (((contract[0],), (contract[1],)), ((), ()))
     return lax.dot_general(left, right, dims, preferred_element_type=jnp.float32)
@@ -27,16 +35,16 @@
 
 def front_kernel(
     n, limits, inv_in, up_in, low_in, index_ref, base_in,
-    x_out, high_out, low_out, last_h, last_l,
-    map_ref, up, inv, low, up_h, up_l, inv_h, inv_l, low_h, low_l, lx_h, lx_l, f_buf, f_h, f_l, x_buf,
+    x_out, high_out, low_out, last_h_out, last_l_out, raw_out, slot_out,
+    map_ref, up, inv, low, up_h, up_l, inv_h, inv_l, low_h, low_l, lx_h, lx_l, f_buf, f_h, f_l, last_h, last_l, x_buf,
     local_sem, part_send, part_recv, up_send, up_recv, inv_send, inv_recv,
     low_send, low_recv, f_send, f_recv, in_sem, out_sem, lx_sem, *packing,
 ):
     packed = limits is not None
     if packed:
         ranks, want, row_want, row_in, c_out, c_in, c_h, c_l, g_h, g_l, c_send, c_recv = packing
-        cap, cross = limits
-        gap = -(-cap // 16) * 16
+        total_cap, far_cap, cross = limits
+        split = total_cap - far_cap
     t = lax.axis_index("tile")
     f = lax.axis_index("front")
     partner = lax.rem(f, 2) * -2 + 1 + f
@@ -90,11 +98,11 @@
             device_id=(partner, t), device_id_type=MESH,
         )
 
-    def hop(kind, child, shard, side):
+    def hop(kind, child, shard, side, source=None):
         send, recv = ((up_send, up_recv), (inv_send, inv_recv), (low_send, low_recv))[kind]
         ref = place(kind, child, shard)
         return pltpu.make_async_remote_copy(
-            src_ref=ref, dst_ref=ref,
+            src_ref=ref if source is None else source, dst_ref=ref,
             send_sem=send.at[side, child, shard], recv_sem=recv.at[child, shard],
             device_id=(f, lax.rem(t + (1 if side == 0 else n - 1), n)), device_id_type=MESH,
         )
@@ -106,14 +114,14 @@
             return t == 0 if side == 0 else t == n - 1
         return t + 1 <= n - 2 if side == 0 else t - 1 >= 1
 
-    def send(kind, child, shard, side):
+    def send(kind, child, shard, side, source=None):
         @pl.when(takes(kind, side))
         def _():
-            hop(kind, child, shard, side).start()
-
-    def send_own(kind, child):
-        send(kind, child, t, 0)
-        send(kind, child, t, 1)
+            hop(kind, child, shard, side, source).start()
+
+    def send_own(kind, child, source=None):
+        send(kind, child, t, 0, source)
+        send(kind, child, t, 1, source)
 
     def pass_on(kinds, child, d, side, where):
         shard = t - d if side == 0 else t + d
@@ -161,7 +169,7 @@
         before = one_hot(before)
         passed = jnp.zeros((8, 1), jnp.float32)
         which = lax.broadcasted_iota(jnp.int32, (8, wc), 0)
-        wants = [jnp.zeros((cap, 8), jnp.float32)] * 2
+        wants = jnp.zeros((total_cap, 8), jnp.float32)
         both = jnp.zeros((8, row_want.shape[2]), jnp.float32)
         inward = jnp.zeros((8, row_in.shape[2]), jnp.float32)
         for s in range(n):
@@ -176,21 +184,21 @@
             digits = jnp.where(which == 0, columns >> 7, jnp.where(which == 1, columns & 127, 1))
             digits = digits.astype(jnp.float32).astype(jnp.bfloat16)
 
-            def pick(q, size, skip=0):
-                return one_hot(lax.broadcasted_iota(jnp.int32, (size, wc), 0) - skip == rank[q:q + 1])
+            def pick(q, size):
+                slot = lax.broadcasted_iota(jnp.int32, (size, wc), 0)
+                return one_hot((total_cap - 1 - slot if q == 1 else slot) == rank[q:q + 1])
 
             for q in range(2):
-                wants[q] = wants[q] + dot(pick(q, cap), digits, (1, 1))
-                both = both + dot(digits, pick(q, both.shape[1], q * gap), (1, 1))
+                wants = wants + dot(pick(q, total_cap), digits, (1, 1))
+                both = both + dot(digits, pick(q, both.shape[1]), (1, 1))
             inward = inward + dot(digits, pick(3, inward.shape[1]), (1, 1))
 
         def across(found):
             value = found[0:1].astype(jnp.int32) * 128 + found[1:2].astype(jnp.int32)
             return jnp.where(found[2:3] > 0, value, -1)
 
-        for q in range(2):
-            found = wants[q].astype(jnp.int32)
-            want[child, q] = jnp.where(found[:, 2:3] > 0, found[:, 0:1] * 128 + found[:, 1:2], -1)
+        found = wants.astype(jnp.int32)
+        want[child] = jnp.where(found[:, 2:3] > 0, found[:, 0:1] * 128 + found[:, 1:2], -1)
         row_want[child] = across(both)
         row_in[child] = across(inward)
 
@@ -278,12 +286,17 @@
     def range_of(start):
         return lax.broadcasted_iota(jnp.int32, (chunk, 1), 0) + start
 
-    groups = 2 if packed else chunks
+    def slots_of(j):
+        return slice(0, split) if j == 0 else slice(split, total_cap)
 
     def end_copy(child, j, target):
-        ref = f_buf.at[child, j]
+        if packed:
+            ref = f_buf.at[child, slots_of(j)]
+            into = raw_out.at[slots_of(j)] if child == 1 else ref
+        else:
+            ref = into = f_buf.at[child, j]
         return pltpu.make_async_remote_copy(
-            src_ref=ref, dst_ref=ref,
+            src_ref=ref, dst_ref=into,
             send_sem=f_send.at[child, j], recv_sem=f_recv.at[child, j],
             device_id=(f, target), device_id_type=MESH,
         )
@@ -299,7 +312,7 @@
         @pl.when(middle)
         def _():
             split_inverse(child)
-            f_buf[child, 0] = factor(child, want[child, 0], far_side=False)
+            f_buf[child, slots_of(0)] = factor(child, want[child, slots_of(0)], far_side=False)
             end_copy(child, 0, end).start()
 
     def serve_far(child):
@@ -312,7 +325,7 @@
             c_l[:cross] = low_part
             c_h[cross:] = rest
             c_l[cross:] = rest
-            f_buf[child, 1] = factor(child, want[child, 1], near_side=False)
+            f_buf[child, slots_of(1)] = factor(child, want[child, slots_of(1)])
             end_copy(child, 1, end).start()
 
     def serve_all(child):
@@ -346,12 +359,9 @@
             if packed:
                 for q in range(2):
                     end_copy(child, q, aside).wait_recv()
-                    high, low_part = parts(f_buf[child, q])
-                    for ref, part in ((g_h, high), (g_l, low_part)):
-                        ref[q * gap:q * gap + cap] = part
-                        stop = gap if q == 0 else ref.shape[0]
-                        if q * gap + cap < stop:
-                            ref[q * gap + cap:stop] = jnp.zeros((stop - q * gap - cap, ref.shape[1]), jnp.bfloat16)
+                if child == 1:
+                    return
+                spread(f_buf[child], (g_h, g_l))
 
             @pl.loop(0, chunks)
             def _(j):
@@ -373,7 +383,7 @@
         rows = pl.ds(pl.multiple_of(lax.rem(i, per) * tall, tall), tall)
         return ref.at[rows, strip(lax.div(i, per))]
 
-    def subtract():
+    def subtract(begin, stop):
         def load(i):
             slot = lax.rem(i, slots)
             return pltpu.make_async_copy(window(base_in, i), x_buf.at[slot], in_sem.at[slot])
@@ -382,17 +392,18 @@
             slot = lax.rem(i, slots)
             return pltpu.make_async_copy(x_buf.at[slot], window(x_out, i), out_sem.at[slot])
 
-        for i in range(ahead):
+        for i in range(begin, min(begin + ahead, stop)):
             load(i).start()
-        take_factor(0)
-
-        @pl.loop(0, blocks)
+        if begin == 0:
+            take_factor(0)
+
+        @pl.loop(begin, stop)
         def _(i):
             j = lax.div(i, per)
 
-            @pl.when(i + ahead < blocks)
+            @pl.when(i + ahead < stop)
             def _():
-                @pl.when(i >= slots - ahead)
+                @pl.when(i >= begin + slots - ahead)
                 def _():
                     store(i - (slots - ahead)).wait()
 
@@ -409,19 +420,23 @@
             x_buf[slot] = x_buf[slot] - total
             store(i).start()
 
-        for i in range(max(blocks - slots, 0), blocks):
+        for i in range(max(stop - slots, begin), stop):
             store(i).wait()
 
     def hand_on(k):
-        return pltpu.make_async_copy((lx_h, lx_l)[k].at[1], (high_out, low_out)[k], lx_sem.at[k])
-
+        if k < 2:
+            return pltpu.make_async_copy((lx_h, lx_l)[k].at[1], (high_out, low_out)[k], lx_sem.at[k])
+        if k < 4:
+            return pltpu.make_async_copy((last_h, last_l)[k - 2], (last_h_out, last_l_out)[k - 2], lx_sem.at[k])
+        return pltpu.make_async_copy(row_want.at[1], slot_out, lx_sem.at[k])
+
+    send_own(2, 0, low_in.at[0])
     for kind in (2, 1, 0):
         exchange(kind).start()
         local(kind).start()
-    local(2).wait()
-    send_own(2, 0)
     exchange(2).wait()
     send_own(2, 1)
+    local(2).wait()
     for kind in (1, 0):
         local(kind).wait()
         exchange(kind).wait()
@@ -436,6 +451,7 @@
     if packed:
         for child in range(2):
             tables(child)
+        hand_on(4).start()
 
     relay_low(0, 1)
     relay_low(1, 1)
@@ -483,17 +499,28 @@
         serve_own(0)
         far(1)
         serve_near(1)
-        subtract()
+        subtract(0, blocks // 2)
         serve_far(1)
+        subtract(blocks // 2, blocks)
+        keeps = middle
     else:
         serve_all(0)
         serve_own(0)
-        subtract()
+        subtract(0, blocks)
         far(1)
         serve_all(1)
+        keeps = t >= 0
     serve_own(1)
     take_factor(1)
-    for k in range(2):
+
+    @pl.when(keeps)
+    def _():
+        for k in (2, 3):
+            hand_on(k).start()
+        for k in (2, 3):
+            hand_on(k).wait()
+
+    for k in (0, 1, 4) if packed else (0, 1):
         hand_on(k).wait()
 
     for child in range(2):
@@ -507,9 +534,13 @@
 
         @pl.when(server)
         def _():
-            @pl.loop(0, groups)
-            def _(j):
-                end_copy(child, j, aside).wait_send()
+            if packed:
+                for j in range(2):
+                    end_copy(child, j, aside).wait_send()
+            else:
+                @pl.loop(0, chunks)
+                def _(j):
+                    end_copy(child, j, aside).wait_send()
 
         if packed:
             @pl.when(middle)
@@ -517,12 +548,16 @@
                 cross_copy(child).wait_send()
 
 
-def capacity(draws, share):
-    spread = math.sqrt(draws * share * (1 - share))
-    return -(-math.ceil(draws * share + 4 * spread) // 8) * 8
-
-
-def assembled(inverse, upper, lower, maps, base, n, limits):
+def capacity(draws, share, order):
+    spread_of = math.sqrt(draws * share * (1 - share) * (1 - draws / order))
+    return -(-math.ceil(draws * share + 4.5 * spread_of) // 8) * 8
+
+
+def padded(rows):
+    return -(-rows // 128) * 128
+
+
+def assembled(inverse, upper, lower, maps, base, n, limits, raw_rows):
     order, width = base.shape
     pivots = inverse.shape[2]
     count = maps.shape[2]
@@ -535,18 +570,17 @@
     slots = 4
     packed = limits is not None
     held, extra = n, []
-    f_shape = (2, chunks, chunk, pivots)
+    f_shape, f_sems = (2, chunks, chunk, pivots), (2, chunks)
     u_shape = (n, pivots, wc)
     if packed:
-        cap, cross = limits
-        cap_pad = -(-(-(-cap // 16) * 16 + cap) // 128) * 128
-        cross_pad = -(-cross // 128) * 128
+        total_cap, _, cross = limits
+        cap_pad, cross_pad = padded(total_cap), padded(cross)
         held = n // 2
-        f_shape = (2, 2, cap, pivots)
+        f_shape, f_sems = (2, total_cap, pivots), (2, 2)
         u_shape = (2, held, pivots, wc)
         extra = [
             vmem((2, 8, count), jnp.int32),
-            vmem((2, 2, cap, 1), jnp.int32),
+            vmem((2, total_cap, 1), jnp.int32),
             vmem((2, 1, cap_pad), jnp.int32),
             vmem((2, 1, cross_pad), jnp.int32),
             vmem((2, cross, pivots), f32),
@@ -562,9 +596,10 @@
         functools.partial(front_kernel, n, limits),
         out_shape=[jax.ShapeDtypeStruct((order, width), f32)]
         + [jax.ShapeDtypeStruct((order, pivots), b16)] * 2
-        + [jax.ShapeDtypeStruct((width, pivots), b16)] * 2,
+        + [jax.ShapeDtypeStruct((width, pivots), b16)] * 2
+        + [jax.ShapeDtypeStruct((raw_rows, pivots), f32), jax.ShapeDtypeStruct((1, padded(raw_rows)), jnp.int32)],
         in_specs=[whole] * 3 + [pl.BlockSpec(memory_space=vmem), whole],
-        out_specs=[whole] * 3 + [pl.BlockSpec(memory_space=vmem)] * 2,
+        out_specs=[whole] * 7,
         scratch_shapes=[
             vmem((2, 1, count), jnp.int32),
             vmem((2, held, pivots, wc), f32),
@@ -581,13 +616,15 @@
             vmem(f_shape, f32),
             vmem((width, pivots), b16),
             vmem((width, pivots), b16),
+            vmem((width, pivots), b16),
+            vmem((width, pivots), b16),
             vmem((slots, min(1024, order), chunk), f32),
             dma((3,)), dma((3,)), dma((3,)),
             dma((2, 2, n)), dma((2, n)),
             dma((2, 2, n)), dma((2, n)),
             dma((2, 2, n)), dma((2, n)),
-            dma(f_shape[:2]), dma(f_shape[:2]),
-            dma((slots,)), dma((slots,)), dma((2,)),
+            dma(f_sems), dma(f_sems),
+            dma((slots,)), dma((slots,)), dma((5,)),
         ] + extra,
         compiler_params=pltpu.CompilerParams(
             collective_id=int(packed), has_side_effects=True, vmem_limit_bytes=63 * 1024 * 1024
@@ -595,31 +632,115 @@
     )(inverse, upper, lower, maps, base)
 
 
-def finish_kernel(x_ref, high_ref, low_ref, f_h, f_l, out_ref):
-    width = out_ref.shape[1]
+def finish_kernel(
+    n, fits_ref, slot_ref, x_in, high_in, low_in, last_h, last_l, raw_in, out,
+    x_buf, high, low, f_h, f_l, raw, g_h, g_l, x_sem, high_sem, low_sem, out_sem, f_sem,
+):
+    t = lax.axis_index("tile")
+    slots, rows, width = x_buf.shape
+    blocks = out.shape[0] // rows
+    ahead = slots // 2
     chunk = min(256, width)
-    for j in range(width // chunk):
-        columns = slice(j * chunk, (j + 1) * chunk)
-        total = dot(high_ref[...], f_h[columns, :], (1, 1))
-        total = total + dot(high_ref[...], f_l[columns, :], (1, 1))
-        total = total + dot(low_ref[...], f_h[columns, :], (1, 1))
-        out_ref[:, columns] = x_ref[:, columns] - total
-
-
-def finished(x, high, low_part, f_h, f_l):
+    expand = (fits_ref[0] > 0) & ((t == 0) | (t == n - 1))
+
+    def loads(i):
+        slot = lax.rem(i, slots)
+        window = pl.ds(pl.multiple_of(i * rows, rows), rows)
+        return [
+            pltpu.make_async_copy(source.at[window], target.at[slot], sem.at[slot])
+            for source, target, sem in ((high_in, high, high_sem), (low_in, low, low_sem), (x_in, x_buf, x_sem))
+        ]
+
+    def store(i):
+        slot = lax.rem(i, slots)
+        window = pl.ds(pl.multiple_of(i * rows, rows), rows)
+        return pltpu.make_async_copy(x_buf.at[slot], out.at[window], out_sem.at[slot])
+
+    packed_copy = pltpu.make_async_copy(raw_in, raw, f_sem.at[0])
+    high_copy = pltpu.make_async_copy(last_h, f_h, f_sem.at[1])
+    low_copy = pltpu.make_async_copy(last_l, f_l, f_sem.at[2])
+
+    @pl.when(expand)
+    def _():
+        packed_copy.start()
+
+    @pl.when(~expand)
+    def _():
+        high_copy.start()
+        low_copy.start()
+
+    for i in range(min(ahead, blocks)):
+        for copy in loads(i):
+            copy.start()
+
+    @pl.when(expand)
+    def _():
+        packed_copy.wait()
+        spread(raw[...], (g_h, g_l))
+
+        @pl.loop(0, width // chunk)
+        def _(j):
+            base = pl.multiple_of(j * chunk, chunk)
+            columns = lax.broadcasted_iota(jnp.int32, (chunk, 1), 0) + (t * width + base)
+            choose = one_hot(columns == slot_ref[...])
+            f_h[pl.ds(base, chunk), :] = dot(choose, g_h[...]).astype(jnp.bfloat16)
+            f_l[pl.ds(base, chunk), :] = dot(choose, g_l[...]).astype(jnp.bfloat16)
+
+    @pl.when(~expand)
+    def _():
+        high_copy.wait()
+        low_copy.wait()
+
+    @pl.loop(0, blocks)
+    def _(i):
+        @pl.when(i + ahead < blocks)
+        def _():
+            @pl.when(i >= slots - ahead)
+            def _():
+                store(i - (slots - ahead)).wait()
+
+            for copy in loads(i + ahead):
+                copy.start()
+
+        for copy in loads(i):
+            copy.wait()
+        slot = lax.rem(i, slots)
+        for j in range(width // chunk):
+            columns = slice(j * chunk, (j + 1) * chunk)
+            total = dot(high[slot], f_h[columns, :], (1, 1))
+            total = total + dot(high[slot], f_l[columns, :], (1, 1))
+            total = total + dot(low[slot], f_h[columns, :], (1, 1))
+            x_buf[slot, :, columns] = x_buf[slot, :, columns] - total
+        store(i).start()
+
+    for i in range(max(blocks - slots, 0), blocks):
+        store(i).wait()
+
+
+def finished(n, fits, x, high, low_part, f_h, f_l, raw, slot):
     order, width = x.shape
-    rows = min(1024, order)
-    tall = pl.BlockSpec((rows, width), lambda i: (i, 0))
-    slim = pl.BlockSpec((rows, high.shape[1]), lambda i: (i, 0))
-    fixed = pl.BlockSpec(f_h.shape, lambda i: (0, 0))
+    pivots = high.shape[1]
+    rows, slots = min(512, order), 4
+    vmem, dma, b16 = pltpu.VMEM, pltpu.SemaphoreType.DMA, jnp.bfloat16
+    whole = pl.BlockSpec(memory_space=pl.ANY)
     return pl.pallas_call(
-        finish_kernel,
+        functools.partial(finish_kernel, n),
         out_shape=jax.ShapeDtypeStruct(x.shape, x.dtype),
-        grid=(order // rows,),
-        in_specs=[tall, slim, slim, fixed, fixed],
-        out_specs=tall,
-        compiler_params=pltpu.CompilerParams(vmem_limit_bytes=40 * 1024 * 1024),
-    )(x, high, low_part, f_h, f_l)
+        in_specs=[pl.BlockSpec(memory_space=pltpu.SMEM), pl.BlockSpec(memory_space=vmem)] + [whole] * 6,
+        out_specs=whole,
+        scratch_shapes=[
+            vmem((slots, rows, width), x.dtype),
+            vmem((slots, rows, pivots), b16),
+            vmem((slots, rows, pivots), b16),
+            vmem((width, pivots), b16),
+            vmem((width, pivots), b16),
+            vmem(raw.shape, raw.dtype),
+            vmem((padded(raw.shape[0]), pivots), b16),
+            vmem((padded(raw.shape[0]), pivots), b16),
+            dma((slots,)), dma((slots,)), dma((slots,)), dma((slots,)), dma((3,)),
+        ],
+        compiler_params=pltpu.CompilerParams(vmem_limit_bytes=60 * 1024 * 1024),
+    )(fits, slot, x, high, low_part, f_h, f_l, raw)
 
 
 def fits_kernel(ranges, index_ref, out_ref):
@@ -627,7 +748,9 @@
     early = lax.broadcasted_iota(jnp.int32, index.shape, 2) < index.shape[2] // 2
     over = None
     for start, stop, is_early, limit in ranges:
-        inside = (index >= start) & (index < stop) & (early if is_early else ~early)
+        inside = (index >= start) & (index < stop)
+        if is_early is not None:
+            inside &= early if is_early else ~early
         extra = jnp.sum(inside.astype(jnp.int32), axis=2, keepdims=True) - limit
         over = extra if over is None else jnp.maximum(over, extra)
     out_ref[0] = (jnp.max(over) <= 0).astype(jnp.int32)
@@ -639,28 +762,30 @@
     count = index_map.shape[2]
     operands = (pivot_inverse[0], panel_upper[0], panel_lower[0], index_map, parent_base[0])
 
+    side = order // 2
+    total = capacity(count, width / order, order)
+    far = capacity(count // 2, width / order, order)
+    cross = capacity(count // 2, 1 / 2, order)
+
     def run(limits, *args):
-        return tuple(assembled(*args, n, limits))
-
-    side = order // 2
-    cap = capacity(count // 2, width / order)
-    cross = capacity(count // 2, 1 / 2)
-    if n != 4 or 2 * cap >= width or cross >= count // 2:
-        return finished(*run(None, *operands))[None]
+        return tuple(assembled(*args, n, limits, total))
+
+    if n != 4 or total >= width or cross >= count // 2:
+        return finished(n, jnp.zeros((1,), jnp.int32), *run(None, *operands))[None]
 
     ranges = (
         (side, order, True, cross), (0, side, False, cross),
-        (0, width, True, cap), (0, width, False, cap),
-        (order - width, order, True, cap), (order - width, order, False, cap),
+        (0, width, None, total), (0, width, False, far),
+        (order - width, order, None, total), (order - width, order, True, far),
     )
     fits = pl.pallas_call(
         functools.partial(fits_kernel, ranges),
         out_shape=jax.ShapeDtypeStruct((1,), jnp.int32),
         in_specs=[pl.BlockSpec(memory_space=pltpu.VMEM)],
         out_specs=pl.BlockSpec(memory_space=pltpu.SMEM),
-    )(index_map)[0]
-    return finished(*lax.cond(
-        fits > 0, functools.partial(run, (cap, cross)), functools.partial(run, None), *operands
+    )(index_map)
+    return finished(n, fits, *lax.cond(
+        fits[0] > 0, functools.partial(run, (total, far, cross)), functools.partial(run, None), *operands
     ))[None]
 
 

time: 225 us -> 218 us (0.969)
  Pallas kernels: 224 us -> 216 us
    pallas_call x1, Pallas kernels: 202 us -> 193 us  [assembled(): pl.pallas_call(functools.partial(front_kernel, n, limits), out_shape=[jax...]
where the time goes in v4:
time: 218 us
  Pallas kernels  216 us (99%)
    pallas_call x1, Pallas kernels, assembled(): pl.pallas_call(functools.partial(front_kernel, n, limits), out_shape=[jax...  193 us
    pallas_call x1, Pallas kernels, finished(): pl.pallas_call(functools.partial(finish_kernel, n), out_shape=jax.ShapeDt...  21.7 us

profile of v4, /device:TPU:0, one launch (start us, length us, event | category | flops | bytes accessed | tf_op | source)
XLA Modules:
  0.0 217.5 jit_solution(4462646751684287107)
XLA Ops:
  0.0 2.0 shard_map.55.fits_ref
  2.7 193.0 %conditional.1 = ((f32[4096,1024]{1,0:T(8,128)}, bf16[4096,512]{1,0:T(8,128)(2,1)}, bf16[4096,512]{1,0:T(8,128)(2,1)}, bf16[1024,512]{1,0:T(8,128)(2,1)}, bf16[1...) conditional(s32[]{:T(128)} %bitcast, (f32[2,128,512]{2,1,0:T(8,128)}, ...), branch_computations={%region_0.0_spmd, %region_1.0_spmd} | conditional | bytes 8 | solution.py:787
  2.7 192.7 %branch_1_fun.1 = (f32[4096,1024]{1,0:T(8,128)}, bf16[4096,512]{1,0:T(8,128)(2,1)}, bf16[4096,512]{1,0:T(8,128)(2,1)}, bf16[1024,512]{1,0:T(8,128)(2,1)}, bf16[1...) custom-call(f32[2,128,512]{2,1,0:T(8,128)} %get-tuple-element.30.inv_in, ...), custom_call_target="tpu_custom_call" | custom-call | tf_op jit(solution)/shard_map/cond/branch_1_fun/pallas_call | solution.py:595
  195.7 21.7 %shard_map.56 = f32[4096,1024]{1,0:T(8,128)} custom-call(s32[1]{0:T(128)} %shard_map.55.fits_ref, s32[1,640]{1,0:T(1,128)S(1)} %get-tuple-element.42.slot_ref, f32[4096,1024]{1,0:T(8,128)} %get-tuple-element.43.x_in, bf16[4096,512]{1,0:T(8,128)(2,1)} %get-tuple-element.44.high_in, bf16[4096,512]{1,0:T(8,128)(2,1)} %get-tuple-element.45.low_in, ...), custom_call_target="tpu_custom_call" | custom-call | tf_op jit(solution)/shard_map/pallas_call | solution.py:726

commit v5 on v4

--- a/solution.py
+++ b/solution.py
@@ -35,10 +35,10 @@
 
 def front_kernel(
     n, limits, inv_in, up_in, low_in, index_ref, base_in,
-    x_out, high_out, low_out, last_h_out, last_l_out, raw_out, slot_out,
-    map_ref, up, inv, low, up_h, up_l, inv_h, inv_l, low_h, low_l, lx_h, lx_l, f_buf, f_h, f_l, last_h, last_l, x_buf,
+    x_out, last_h_out, last_l_out, late_out,
+    map_ref, up, inv, low, up_h, up_l, inv_h, inv_l, low_h, low_l, lx_h, lx_l, f_buf, f_h, f_l, x_buf,
     local_sem, part_send, part_recv, up_send, up_recv, inv_send, inv_recv,
-    low_send, low_recv, f_send, f_recv, in_sem, out_sem, lx_sem, *packing,
+    low_send, low_recv, f_send, f_recv, in_sem, out_sem, out_copy_sem, *packing,
 ):
     packed = limits is not None
     if packed:
@@ -136,6 +136,14 @@
     def relay_low(child, d):
         pass_on((2,), child, d, 0, t >= 0)
         pass_on((2,), child, d, 1, t >= 0)
+
+    def inner(child, d, where):
+        pass_on((2,), child, d, 1, where & lower)
+        pass_on((2,), child, d, 0, where & (t >= n // 2))
+
+    def outer(child, d):
+        pass_on((2,), child, d, 0, middle & lower)
+        pass_on((2,), child, d, 1, middle & (t >= n // 2))
 
     kinds = (1,) if packed else (1, 0)
 
@@ -235,7 +243,11 @@
             cross_copy(child).start()
 
     def place_rows(child):
-        @pl.loop(0, n)
+        held = (n - 1 if packed and child == 1 else n) * lr
+        from_shard = jnp.where(lower, 0, 1) if packed and child == 1 else 0
+        used = pl.ds(pl.multiple_of(from_shard * lr, lr), held)
+
+        @pl.loop(from_shard, from_shard + held // lr)
         def _(s):
             rows = pl.ds(pl.multiple_of(s * lr, lr), lr)
             high, low_part = parts(low[child, s])
@@ -247,10 +259,10 @@
         @pl.loop(0, order // span)
         def _(j):
             base = pl.multiple_of(j * span, span)
-            rows = lax.broadcasted_iota(jnp.int32, (span, count), 0) + base
-            choose = one_hot(rows == map_ref[child])
-            lx_h[child, pl.ds(base, span), :] = dot(choose, low_h[...]).astype(jnp.bfloat16)
-            lx_l[child, pl.ds(base, span), :] = dot(choose, low_l[...]).astype(jnp.bfloat16)
+            rows = lax.broadcasted_iota(jnp.int32, (span, held), 0) + base
+            choose = one_hot(rows == map_ref[child, :, used])
+            lx_h[child, pl.ds(base, span), :] = dot(choose, low_h[used, :]).astype(jnp.bfloat16)
+            lx_l[child, pl.ds(base, span), :] = dot(choose, low_l[used, :]).astype(jnp.bfloat16)
 
     def split_inverse(child):
         @pl.loop(0, n)
@@ -292,21 +304,17 @@
     def end_copy(child, j, target):
         if packed:
             ref = f_buf.at[child, slots_of(j)]
-            into = raw_out.at[slots_of(j)] if child == 1 else ref
         else:
-            ref = into = f_buf.at[child, j]
+            ref = f_buf.at[child, j]
         return pltpu.make_async_remote_copy(
-            src_ref=ref, dst_ref=into,
+            src_ref=ref, dst_ref=ref,
             send_sem=f_send.at[child, j], recv_sem=f_recv.at[child, j],
             device_id=(f, target), device_id_type=MESH,
         )
 
-    def kept(child):
-        return (f_h, f_l) if child == 0 else (last_h, last_l)
-
     def keep(child, j, value):
-        for ref, part in zip(kept(child), parts(value)):
-            ref[strip(j), :] = part
+        for ref, part in zip((f_h, f_l), parts(value)):
+            ref[child, strip(j), :] = part
 
     def serve_near(child):
         @pl.when(middle)
@@ -359,16 +367,14 @@
             if packed:
                 for q in range(2):
                     end_copy(child, q, aside).wait_recv()
-                if child == 1:
-                    return
                 spread(f_buf[child], (g_h, g_l))
 
             @pl.loop(0, chunks)
             def _(j):
                 if packed:
                     choose = one_hot(range_of(t * width + j * chunk) == row_want[child])
-                    for ref, source in zip(kept(child), (g_h, g_l)):
-                        ref[strip(j), :] = dot(choose, source[...]).astype(jnp.bfloat16)
+                    for ref, source in ((f_h, g_h), (f_l, g_l)):
+                        ref[child, strip(j), :] = dot(choose, source[...]).astype(jnp.bfloat16)
                 else:
                     end_copy(child, j, aside).wait_recv()
                     keep(child, j, f_buf[child, j])
@@ -383,10 +389,12 @@
         rows = pl.ds(pl.multiple_of(lax.rem(i, per) * tall, tall), tall)
         return ref.at[rows, strip(lax.div(i, per))]
 
-    def subtract(begin, stop):
+    def subtract(child, begin, stop):
+        source = base_in if child == 0 else x_out
+
         def load(i):
             slot = lax.rem(i, slots)
-            return pltpu.make_async_copy(window(base_in, i), x_buf.at[slot], in_sem.at[slot])
+            return pltpu.make_async_copy(window(source, i), x_buf.at[slot], in_sem.at[slot])
 
         def store(i):
             slot = lax.rem(i, slots)
@@ -395,7 +403,7 @@
         for i in range(begin, min(begin + ahead, stop)):
             load(i).start()
         if begin == 0:
-            take_factor(0)
+            take_factor(child)
 
         @pl.loop(begin, stop)
         def _(i):
@@ -410,11 +418,11 @@
                 load(i + ahead).start()
 
             rows = pl.ds(pl.multiple_of(lax.rem(i, per) * tall, tall), tall)
-            high = f_h[strip(j), :]
-            left = lx_h[0, rows, :]
+            high = f_h[child, strip(j), :]
+            left = lx_h[child, rows, :]
             total = dot(left, high, (1, 1))
-            total = total + dot(left, f_l[strip(j), :], (1, 1))
-            total = total + dot(lx_l[0, rows, :], high, (1, 1))
+            total = total + dot(left, f_l[child, strip(j), :], (1, 1))
+            total = total + dot(lx_l[child, rows, :], high, (1, 1))
             load(i).wait()
             slot = lax.rem(i, slots)
             x_buf[slot] = x_buf[slot] - total
@@ -425,17 +433,20 @@
 
     def hand_on(k):
         if k < 2:
-            return pltpu.make_async_copy((lx_h, lx_l)[k].at[1], (high_out, low_out)[k], lx_sem.at[k])
-        if k < 4:
-            return pltpu.make_async_copy((last_h, last_l)[k - 2], (last_h_out, last_l_out)[k - 2], lx_sem.at[k])
-        return pltpu.make_async_copy(row_want.at[1], slot_out, lx_sem.at[k])
-
+            return pltpu.make_async_copy((f_h, f_l)[k].at[1], (last_h_out, last_l_out)[k], out_copy_sem.at[k])
+        return pltpu.make_async_copy(low.at[1, late], late_out, out_copy_sem.at[k])
+
+    late = jnp.where(lower, n - 1, 0) if packed else 0
     send_own(2, 0, low_in.at[0])
     for kind in (2, 1, 0):
         exchange(kind).start()
         local(kind).start()
     exchange(2).wait()
-    send_own(2, 1)
+
+    @pl.when(middle if packed else t >= 0)
+    def _():
+        send_own(2, 1)
+
     local(2).wait()
     for kind in (1, 0):
         local(kind).wait()
@@ -443,30 +454,78 @@
 
     @pl.when(at_end)
     def _():
-        for kind, child in ((1, 0), (1, 1), (0, 0), (0, 1)) if packed else ((1, 0), (0, 0), (1, 1), (0, 1)):
-            send_own(kind, child)
+        for child in range(2):
+            for kind in (1, 0):
+                send_own(kind, child)
+        if packed:
+            send_own(2, 1)
 
     for child in range(2):
         map_ref[child] = index_ref[f if child == 0 else partner, child:child + 1, :]
     if packed:
         for child in range(2):
             tables(child)
-        hand_on(4).start()
-
-    relay_low(0, 1)
-    relay_low(1, 1)
-
-    @pl.when(middle)
-    def _():
-        for kind, child in ((1, 0), (1, 1)) if packed else ((1, 0), (0, 0)):
-            send_own(kind, child)
-
-    if packed:
-        near(0)
-        near(1)
-        relay_low(0, 2)
-        pack(0)
+
+        @pl.when(middle)
+        def _():
+            outer(0, 1)
+            inner(0, 1, middle)
+            send_own(1, 0)
+            near(0)
+            inner(1, 1, middle)
+            pack(0)
+            send_own(1, 1)
+            near(1)
+            inner(0, 2, middle)
+
+        @pl.when(at_end)
+        def _():
+            for child, d in ((0, 1), (1, 1), (0, 2), (1, 2), (0, 3)):
+                inner(child, d, at_end)
+
+        place_rows(0)
+
+        @pl.when(middle)
+        def _():
+            pack(1)
+            far(0)
+            serve_near(0)
+            outer(1, 1)
+            serve_far(0)
+            serve_own(0)
+
+        place_rows(1)
+
+        @pl.when(middle)
+        def _():
+            far(1)
+            serve_near(1)
+
+        subtract(0, 0, blocks // 2)
+
+        @pl.when(middle)
+        def _():
+            serve_far(1)
+            serve_own(1)
+
+        subtract(0, blocks // 2, blocks)
+        inner(1, 2, middle)
+        subtract(1, 0, blocks)
+        for k in range(2):
+            hand_on(k).start()
+        inner(1, 3, at_end)
+        hand_on(2).start()
+        for k in range(3):
+            hand_on(k).wait()
     else:
+        relay_low(0, 1)
+        relay_low(1, 1)
+
+        @pl.when(middle)
+        def _():
+            send_own(1, 0)
+            send_own(0, 0)
+
         relay_low(0, 2)
         near(0)
 
@@ -475,53 +534,24 @@
             send_own(1, 1)
             send_own(0, 1)
 
-    relay_low(1, 2)
-
-    @pl.loop(3, n - 1)
-    def _(d):
-        relay_low(0, d)
-        relay_low(1, d)
-
-    relay_low(0, n - 1)
-    place_rows(0)
-    if packed:
-        pack(1)
-    else:
+        relay_low(1, 2)
+
+        @pl.loop(3, n)
+        def _(d):
+            relay_low(0, d)
+            relay_low(1, d)
+
         near(1)
-    relay_low(1, n - 1)
-    place_rows(1)
-    for k in range(2):
-        hand_on(k).start()
-    far(0)
-    if packed:
-        serve_near(0)
-        serve_far(0)
-        serve_own(0)
-        far(1)
-        serve_near(1)
-        subtract(0, blocks // 2)
-        serve_far(1)
-        subtract(blocks // 2, blocks)
-        keeps = middle
-    else:
-        serve_all(0)
-        serve_own(0)
-        subtract(0, blocks)
-        far(1)
-        serve_all(1)
-        keeps = t >= 0
-    serve_own(1)
-    take_factor(1)
-
-    @pl.when(keeps)
-    def _():
-        for k in (2, 3):
+        place_rows(0)
+        place_rows(1)
+        for child in range(2):
+            far(child)
+            serve_all(child)
+            serve_own(child)
+            subtract(child, 0, blocks)
+        for k in range(2):
             hand_on(k).start()
-        for k in (2, 3):
             hand_on(k).wait()
-
-    for k in (0, 1, 4) if packed else (0, 1):
-        hand_on(k).wait()
 
     for child in range(2):
         @pl.loop(0, n)
@@ -547,6 +577,11 @@
             def _():
                 cross_copy(child).wait_send()
 
+    if not packed:
+        low[1, late] = jnp.zeros(late_out.shape, jnp.float32)
+        hand_on(2).start()
+        hand_on(2).wait()
+
 
 def capacity(draws, share, order):
     spread_of = math.sqrt(draws * share * (1 - share) * (1 - draws / order))
@@ -557,7 +592,7 @@
     return -(-rows // 128) * 128
 
 
-def assembled(inverse, upper, lower, maps, base, n, limits, raw_rows):
+def assembled(inverse, upper, lower, maps, base, n, limits):
     order, width = base.shape
     pivots = inverse.shape[2]
     count = maps.shape[2]
@@ -595,11 +630,10 @@
     return pl.pallas_call(
         functools.partial(front_kernel, n, limits),
         out_shape=[jax.ShapeDtypeStruct((order, width), f32)]
-        + [jax.ShapeDtypeStruct((order, pivots), b16)] * 2
         + [jax.ShapeDtypeStruct((width, pivots), b16)] * 2
-        + [jax.ShapeDtypeStruct((raw_rows, pivots), f32), jax.ShapeDtypeStruct((1, padded(raw_rows)), jnp.int32)],
+        + [jax.ShapeDtypeStruct((lr, pivots), f32)],
         in_specs=[whole] * 3 + [pl.BlockSpec(memory_space=vmem), whole],
-        out_specs=[whole] * 7,
+        out_specs=[whole] * 4,
         scratch_shapes=[
             vmem((2, 1, count), jnp.int32),
             vmem((2, held, pivots, wc), f32),
@@ -614,17 +648,15 @@
             vmem((2, order, pivots), b16),
             vmem((2, order, pivots), b16),
             vmem(f_shape, f32),
-            vmem((width, pivots), b16),
-            vmem((width, pivots), b16),
-            vmem((width, pivots), b16),
-            vmem((width, pivots), b16),
+            vmem((2, width, pivots), b16),
+            vmem((2, width, pivots), b16),
             vmem((slots, min(1024, order), chunk), f32),
             dma((3,)), dma((3,)), dma((3,)),
             dma((2, 2, n)), dma((2, n)),
             dma((2, 2, n)), dma((2, n)),
             dma((2, 2, n)), dma((2, n)),
             dma(f_sems), dma(f_sems),
-            dma((slots,)), dma((slots,)), dma((5,)),
+            dma((slots,)), dma((slots,)), dma((3,)),
         ] + extra,
         compiler_params=pltpu.CompilerParams(
             collective_id=int(packed), has_side_effects=True, vmem_limit_bytes=63 * 1024 * 1024
@@ -633,63 +665,48 @@
 
 
 def finish_kernel(
-    n, fits_ref, slot_ref, x_in, high_in, low_in, last_h, last_l, raw_in, out,
-    x_buf, high, low, f_h, f_l, raw, g_h, g_l, x_sem, high_sem, low_sem, out_sem, f_sem,
+    n, index_ref, x_in, last_h, last_l, late_in, out,
+    x_buf, f_h, f_l, late, u_h, u_l, x_sem, out_sem, f_sem,
 ):
     t = lax.axis_index("tile")
+    f = lax.axis_index("front")
+    partner = lax.rem(f, 2) * -2 + 1 + f
     slots, rows, width = x_buf.shape
+    lr = late.shape[0]
     blocks = out.shape[0] // rows
     ahead = slots // 2
     chunk = min(256, width)
-    expand = (fits_ref[0] > 0) & ((t == 0) | (t == n - 1))
-
-    def loads(i):
+    shard = jnp.where(t < n // 2, n - 1, 0)
+    places = index_ref[partner, 1:2, pl.ds(pl.multiple_of(shard * lr, lr), lr)]
+
+    def window(i):
+        return pl.ds(pl.multiple_of(i * rows, rows), rows)
+
+    def load(i):
         slot = lax.rem(i, slots)
-        window = pl.ds(pl.multiple_of(i * rows, rows), rows)
-        return [
-            pltpu.make_async_copy(source.at[window], target.at[slot], sem.at[slot])
-            for source, target, sem in ((high_in, high, high_sem), (low_in, low, low_sem), (x_in, x_buf, x_sem))
-        ]
+        return pltpu.make_async_copy(x_in.at[window(i)], x_buf.at[slot], x_sem.at[slot])
 
     def store(i):
         slot = lax.rem(i, slots)
-        window = pl.ds(pl.multiple_of(i * rows, rows), rows)
-        return pltpu.make_async_copy(x_buf.at[slot], out.at[window], out_sem.at[slot])
-
-    packed_copy = pltpu.make_async_copy(raw_in, raw, f_sem.at[0])
-    high_copy = pltpu.make_async_copy(last_h, f_h, f_sem.at[1])
-    low_copy = pltpu.make_async_copy(last_l, f_l, f_sem.at[2])
-
-    @pl.when(expand)
-    def _():
-        packed_copy.start()
-
-    @pl.when(~expand)
-    def _():
-        high_copy.start()
-        low_copy.start()
-
+        return pltpu.make_async_copy(x_buf.at[slot], out.at[window(i)], out_sem.at[slot])
+
+    first = [
+        pltpu.make_async_copy(source, target, f_sem.at[k])
+        for k, (source, target) in enumerate(((late_in, late), (last_h, f_h), (last_l, f_l)))
+    ]
+    for copy in first:
+        copy.start()
     for i in range(min(ahead, blocks)):
-        for copy in loads(i):
-            copy.start()
-
-    @pl.when(expand)
-    def _():
-        packed_copy.wait()
-        spread(raw[...], (g_h, g_l))
-
-        @pl.loop(0, width // chunk)
-        def _(j):
-            base = pl.multiple_of(j * chunk, chunk)
-            columns = lax.broadcasted_iota(jnp.int32, (chunk, 1), 0) + (t * width + base)
-            choose = one_hot(columns == slot_ref[...])
-            f_h[pl.ds(base, chunk), :] = dot(choose, g_h[...]).astype(jnp.bfloat16)
-            f_l[pl.ds(base, chunk), :] = dot(choose, g_l[...]).astype(jnp.bfloat16)
-
-    @pl.when(~expand)
-    def _():
-        high_copy.wait()
-        low_copy.wait()
+        load(i).start()
+    for copy in first:
+        copy.wait()
+    left = parts(late[...])
+    for j in range(width // chunk):
+        columns = slice(j * chunk, (j + 1) * chunk)
+        total = dot(left[0], f_h[columns, :], (1, 1))
+        total = total + dot(left[0], f_l[columns, :], (1, 1))
+        total = total + dot(left[1], f_h[columns, :], (1, 1))
+        u_h[:, columns], u_l[:, columns] = parts(total)
 
     @pl.loop(0, blocks)
     def _(i):
@@ -699,17 +716,14 @@
             def _():
                 store(i - (slots - ahead)).wait()
 
-            for copy in loads(i + ahead):
-                copy.start()
-
-        for copy in loads(i):
-            copy.wait()
+            load(i + ahead).start()
+
+        choose = one_hot(lax.broadcasted_iota(jnp.int32, (rows, lr), 0) + i * rows == places)
+        load(i).wait()
         slot = lax.rem(i, slots)
         for j in range(width // chunk):
             columns = slice(j * chunk, (j + 1) * chunk)
-            total = dot(high[slot], f_h[columns, :], (1, 1))
-            total = total + dot(high[slot], f_l[columns, :], (1, 1))
-            total = total + dot(low[slot], f_h[columns, :], (1, 1))
+            total = dot(choose, u_h[:, columns]) + dot(choose, u_l[:, columns])
             x_buf[slot, :, columns] = x_buf[slot, :, columns] - total
         store(i).start()
 
@@ -717,30 +731,27 @@
         store(i).wait()
 
 
-def finished(n, fits, x, high, low_part, f_h, f_l, raw, slot):
+def finished(n, index_map, x, f_h, f_l, late):
     order, width = x.shape
-    pivots = high.shape[1]
     rows, slots = min(512, order), 4
     vmem, dma, b16 = pltpu.VMEM, pltpu.SemaphoreType.DMA, jnp.bfloat16
     whole = pl.BlockSpec(memory_space=pl.ANY)
     return pl.pallas_call(
         functools.partial(finish_kernel, n),
         out_shape=jax.ShapeDtypeStruct(x.shape, x.dtype),
-        in_specs=[pl.BlockSpec(memory_space=pltpu.SMEM), pl.BlockSpec(memory_space=vmem)] + [whole] * 6,
+        in_specs=[pl.BlockSpec(memory_space=vmem)] + [whole] * 4,
         out_specs=whole,
         scratch_shapes=[
             vmem((slots, rows, width), x.dtype),
-            vmem((slots, rows, pivots), b16),
-            vmem((slots, rows, pivots), b16),
-            vmem((width, pivots), b16),
-            vmem((width, pivots), b16),
-            vmem(raw.shape, raw.dtype),
-            vmem((padded(raw.shape[0]), pivots), b16),
-            vmem((padded(raw.shape[0]), pivots), b16),
-            dma((slots,)), dma((slots,)), dma((slots,)), dma((slots,)), dma((3,)),
+            vmem(f_h.shape, b16),
+            vmem(f_h.shape, b16),
+            vmem(late.shape, late.dtype),
+            vmem((late.shape[0], width), b16),
+            vmem((late.shape[0], width), b16),
+            dma((slots,)), dma((slots,)), dma((3,)),
         ],
         compiler_params=pltpu.CompilerParams(vmem_limit_bytes=60 * 1024 * 1024),
-    )(fits, slot, x, high, low_part, f_h, f_l, raw)
+    )(index_map, x, f_h, f_l, late)
 
 
 def fits_kernel(ranges, index_ref, out_ref):
@@ -768,10 +779,10 @@
     cross = capacity(count // 2, 1 / 2, order)
 
     def run(limits, *args):
-        return tuple(assembled(*args, n, limits, total))
+        return tuple(assembled(*args, n, limits))
 
     if n != 4 or total >= width or cross >= count // 2:
-        return finished(n, jnp.zeros((1,), jnp.int32), *run(None, *operands))[None]
+        return finished(n, index_map, *run(None, *operands))[None]
 
     ranges = (
         (side, order, True, cross), (0, side, False, cross),
@@ -784,7 +795,7 @@
         in_specs=[pl.BlockSpec(memory_space=pltpu.VMEM)],
         out_specs=pl.BlockSpec(memory_space=pltpu.SMEM),
     )(index_map)
-    return finished(n, fits, *lax.cond(
+    return finished(n, index_map, *lax.cond(
         fits[0] > 0, functools.partial(run, (total, far, cross)), functools.partial(run, None), *operands
     ))[None]
 

time: 218 us -> 221 us (1.014)
  Pallas kernels: 216 us -> 220 us
    pallas_call x1, Pallas kernels: 193 us -> 200 us  [assembled(): pl.pallas_call(functools.partial(front_kernel, n, limits), out_shape=[jax...]
    pallas_call x1, Pallas kernels: 21.7 us -> 17.3 us  [finished(): pl.pallas_call(functools.partial(finish_kernel, n), out_shape=jax.ShapeDt...]
where the time goes in v5:
time: 221 us
  Pallas kernels  220 us (100%)
    pallas_call x1, Pallas kernels, assembled(): pl.pallas_call(functools.partial(front_kernel, n, limits), out_shape=[jax...  200 us
    pallas_call x1, Pallas kernels, finished(): pl.pallas_call(functools.partial(finish_kernel, n), out_shape=jax.ShapeDt...  17.3 us

profile of v5, /device:TPU:0, one launch (start us, length us, event | category | flops | bytes accessed | tf_op | source)
XLA Modules:
  0.0 220.7 jit_solution(11177598998179354332)
XLA Ops:
  0.0 2.0 shard_map.55
  2.7 200.5 %conditional.1 = ((f32[4096,1024]{1,0:T(8,128)}, bf16[1024,512]{1,0:T(8,128)(2,1)}, bf16[1024,512]{1,0:T(8,128)(2,1)}, f32[512,512]{1,0:T(8,128)})) conditional(s32[]{:T(128)} %bitcast, (f32[2,128,512]{2,1,0:T(8,128)}, f32[2,512,512]{2,1,0:T(8,128)}, f32[2,512,512]{2,1,0:T(8,128)}, s32[8,2,2048]{2,1,0:T(2,128)}, f32[4096,1024]{1,0:T(8,128)}) %tuple.22, ...), branch_computations={%region_0.0_spmd, %region_1.0_spmd} | conditional | bytes 8 | solution.py:798
  2.7 200.2 %branch_1_fun.1 = (f32[4096,1024]{1,0:T(8,128)}, bf16[1024,512]{1,0:T(8,128)(2,1)}, bf16[1024,512]{1,0:T(8,128)(2,1)}, f32[512,512]{1,0:T(8,128)}) custom-call(f32[2,128,512]{2,1,0:T(8,128)} %get-tuple-element.30.inv_in, f32[2,512,512]{2,1,0:T(8,128)} %get-tuple-element.31.up_in, f32[2,512,512]{2,1,0:T(8,128)} %get-tuple-element.32.low_in, ...), custom_call_target="tpu_custom_call" | custom-call | tf_op jit(solution)/shard_map/cond/branch_1_fun/pallas_call | solution.py:630
  203.2 17.3 %shard_map.56 = f32[4096,1024]{1,0:T(8,128)} custom-call(s32[8,2,2048]{2,1,0:T(2,128)} %index_ref.3, f32[4096,1024]{1,0:T(8,128)} %get-tuple-element.39.x_in, bf16[1024,512]{1,0:T(8,128)(2,1)} %get-tuple-element.40.last_h, bf16[1024,512]{1,0:T(8,128)(2,1)} %get-tuple-element.41.last_l, f32[512,512]{1,0:T(8,128)} %get-tuple-element.42.late_in), custom_call_target="tpu_custom_call" | custom-call | tf_op jit(solution)/shard_map/pallas_call | solution.py:739

commit v6 on v5

--- a/solution.py
+++ b/solution.py
@@ -232,14 +232,20 @@
                 high, low_part = parts(up[child, k])
                 up_h[child, k] = high
                 up_l[child, k] = low_part
-            total = None
-            for k in range(n // 2):
-                shard = pl.ds(pl.multiple_of((first + k) * wc, wc), wc)
-                rank = ranks[child, 2:3, shard]
-                choose = one_hot(lax.broadcasted_iota(jnp.int32, (cross, wc), 0) == rank)
-                piece = dot(choose, up_h[child, k], (1, 1)) + dot(choose, up_l[child, k], (1, 1))
-                total = piece if total is None else total + piece
-            c_out[child] = total
+            step = cross // 4 if cross % 32 == 0 else cross
+
+            @pl.loop(0, cross // step)
+            def _(j):
+                base = pl.multiple_of(j * step, 8)
+                total = None
+                for k in range(n // 2):
+                    shard = pl.ds(pl.multiple_of((first + k) * wc, wc), wc)
+                    rank = ranks[child, 2:3, shard] - base
+                    choose = one_hot(lax.broadcasted_iota(jnp.int32, (step, wc), 0) == rank)
+                    piece = dot(choose, up_h[child, k], (1, 1)) + dot(choose, up_l[child, k], (1, 1))
+                    total = piece if total is None else total + piece
+                c_out[child, pl.ds(base, step), :] = total
+
             cross_copy(child).start()
 
     def place_rows(child):
@@ -463,8 +469,7 @@
     for child in range(2):
         map_ref[child] = index_ref[f if child == 0 else partner, child:child + 1, :]
     if packed:
-        for child in range(2):
-            tables(child)
+        pl.loop(0, 2)(tables)
 
         @pl.when(middle)
         def _():
@@ -480,8 +485,10 @@
 
         @pl.when(at_end)
         def _():
-            for child, d in ((0, 1), (1, 1), (0, 2), (1, 2), (0, 3)):
+            for child, d in ((0, 1), (1, 1), (0, 2), (1, 2)):
                 inner(child, d, at_end)
+            place_rows(1)
+            inner(0, 3, at_end)
 
         place_rows(0)
 
@@ -493,11 +500,7 @@
             outer(1, 1)
             serve_far(0)
             serve_own(0)
-
-        place_rows(1)
-
-        @pl.when(middle)
-        def _():
+            place_rows(1)
             far(1)
             serve_near(1)
 
@@ -696,10 +699,10 @@
     ]
     for copy in first:
         copy.start()
+    for copy in first:
+        copy.wait()
     for i in range(min(ahead, blocks)):
         load(i).start()
-    for copy in first:
-        copy.wait()
     left = parts(late[...])
     for j in range(width // chunk):
         columns = slice(j * chunk, (j + 1) * chunk)

time: 221 us -> 215 us (0.973)
  Pallas kernels: 220 us -> 214 us
    pallas_call x1, Pallas kernels: 200 us -> 195 us  [assembled(): pl.pallas_call(functools.partial(front_kernel, n, limits), out_shape=[jax...]
where the time goes in v6:
time: 215 us
  Pallas kernels  214 us (100%)
    pallas_call x1, Pallas kernels, assembled(): pl.pallas_call(functools.partial(front_kernel, n, limits), out_shape=[jax...  195 us
    pallas_call x1, Pallas kernels, finished(): pl.pallas_call(functools.partial(finish_kernel, n), out_shape=jax.ShapeDt...  16.7 us

profile of v6, /device:TPU:0, one launch (start us, length us, event | category | flops | bytes accessed | tf_op | source)
XLA Modules:
  0.0 214.7 jit_solution(1124202834769373758)
XLA Ops:
  0.0 2.0 shard_map.55
  2.7 195.2 %conditional.1 = ((f32[4096,1024]{1,0:T(8,128)}, bf16[1024,512]{1,0:T(8,128)(2,1)}, bf16[1024,512]{1,0:T(8,128)(2,1)}, f32[512,512]{1,0:T(8,128)})) conditional(s32[]{:T(128)} %bitcast, (f32[2,128,512]{2,1,0:T(8,128)}, f32[2,512,512]{2,1,0:T(8,128)}, f32[2,512,512]{2,1,0:T(8,128)}, s32[8,2,2048]{2,1,0:T(2,128)}, f32[4096,1024]{1,0:T(8,128)}) %tuple.22, ...), branch_computations={%region_0.0_spmd, %region_1.0_spmd} | conditional | bytes 8 | solution.py:801
  2.7 194.9 %branch_1_fun.1 = (f32[4096,1024]{1,0:T(8,128)}, bf16[1024,512]{1,0:T(8,128)(2,1)}, bf16[1024,512]{1,0:T(8,128)(2,1)}, f32[512,512]{1,0:T(8,128)}) custom-call(f32[2,128,512]{2,1,0:T(8,128)} %get-tuple-element.30.inv_in, f32[2,512,512]{2,1,0:T(8,128)} %get-tuple-element.31.up_in, f32[2,512,512]{2,1,0:T(8,128)} %get-tuple-element.32.low_in, ...), custom_call_target="tpu_custom_call" | custom-call | tf_op jit(solution)/shard_map/cond/branch_1_fun/pallas_call | solution.py:633
  197.9 16.7 %shard_map.56 = f32[4096,1024]{1,0:T(8,128)} custom-call(s32[8,2,2048]{2,1,0:T(2,128)} %index_ref.3, f32[4096,1024]{1,0:T(8,128)} %get-tuple-element.39.x_in, bf16[1024,512]{1,0:T(8,128)(2,1)} %get-tuple-element.40.last_h, bf16[1024,512]{1,0:T(8,128)(2,1)} %get-tuple-element.41.last_l, f32[512,512]{1,0:T(8,128)} %get-tuple-element.42.late_in), custom_call_target="tpu_custom_call" | custom-call | tf_op jit(solution)/shard_map/pallas_call | solution.py:742

commit v7 on v6

--- a/solution.py
+++ b/solution.py
@@ -33,16 +33,39 @@
     return match.astype(jnp.float32).astype(jnp.bfloat16)
 
 
+def counts_fit(index_ref, order, width, limits):
+    total_cap, far_cap, cross = limits
+    half = index_ref.shape[2] // 2
+
+    def number(early, test):
+        part = index_ref[:, :, :half] if early else index_ref[:, :, half:]
+        return jnp.sum(test(part).astype(jnp.int32), axis=2, keepdims=True)
+
+    def first(m):
+        return m < width
+
+    def last(m):
+        return m >= order - width
+
+    over = number(True, lambda m: m >= order // 2) - cross
+    over = jnp.maximum(over, number(False, lambda m: m < order // 2) - cross)
+    for test, far_early in ((first, False), (last, True)):
+        far = number(far_early, test)
+        over = jnp.maximum(over, far - far_cap)
+        over = jnp.maximum(over, far + number(not far_early, test) - total_cap)
+    return (jnp.max(over) <= 0).astype(jnp.int32)
+
+
 def front_kernel(
     n, limits, inv_in, up_in, low_in, index_ref, base_in,
-    x_out, last_h_out, last_l_out, late_out,
-    map_ref, up, inv, low, up_h, up_l, inv_h, inv_l, low_h, low_l, lx_h, lx_l, f_buf, f_h, f_l, x_buf,
+    x_out, u_h_out, u_l_out, fits_out,
+    map_ref, up, inv, low, up_h, up_l, inv_h, inv_l, low_h, low_l, lx_h, lx_l, f_buf, f_h, f_l, u_h, u_l, x_buf,
     local_sem, part_send, part_recv, up_send, up_recv, inv_send, inv_recv,
     low_send, low_recv, f_send, f_recv, in_sem, out_sem, out_copy_sem, *packing,
 ):
     packed = limits is not None
     if packed:
-        ranks, want, row_want, row_in, c_out, c_in, c_h, c_l, g_h, g_l, c_send, c_recv = packing
+        ranks, want, row_want, row_in, c_out, c_in, c_h, c_l, g_h, g_l, c_send, c_recv, late_send, late_recv = packing
         total_cap, far_cap, cross = limits
         split = total_cap - far_cap
     t = lax.axis_index("tile")
@@ -438,11 +461,52 @@
             store(i).wait()
 
     def hand_on(k):
-        if k < 2:
-            return pltpu.make_async_copy((f_h, f_l)[k].at[1], (last_h_out, last_l_out)[k], out_copy_sem.at[k])
-        return pltpu.make_async_copy(low.at[1, late], late_out, out_copy_sem.at[k])
-
-    late = jnp.where(lower, n - 1, 0) if packed else 0
+        return pltpu.make_async_copy((u_h, u_l)[k], (u_h_out, u_l_out)[k], out_copy_sem.at[k])
+
+    late = jnp.where(lower, n - 1, 0)
+
+    def late_rows(k):
+        return slice(k * (lr // 2), (k + 1) * (lr // 2))
+
+    def late_copy(k, target):
+        ref = low.at[1, late, late_rows(k)]
+        return pltpu.make_async_remote_copy(
+            src_ref=ref, dst_ref=ref, send_sem=late_send.at[k], recv_sem=late_recv.at[k],
+            device_id=(f, target), device_id_type=MESH,
+        )
+
+    def take_late():
+        @pl.when(middle)
+        def _():
+            @pl.when(lower)
+            def _():
+                hop(2, 1, n - 1, 1).wait_recv()
+
+            @pl.when(t >= n // 2)
+            def _():
+                hop(2, 1, 0, 0).wait_recv()
+
+            for k in range(2):
+                late_copy(k, end).start()
+
+    def last_update():
+        @pl.loop(0, 2)
+        def _(k):
+            @pl.when(at_end)
+            def _():
+                for q in range(2):
+                    @pl.when(k == q)
+                    def _():
+                        late_copy(q, aside).wait_recv()
+
+            rows = pl.ds(pl.multiple_of(k * (lr // 2), lr // 2), lr // 2)
+            left = parts(low[1, late, rows, :])
+            for j in range(chunks):
+                columns = slice(j * chunk, (j + 1) * chunk)
+                total = dot(left[0], f_h[1, columns, :], (1, 1))
+                total = total + dot(left[0], f_l[1, columns, :], (1, 1))
+                total = total + dot(left[1], f_h[1, columns, :], (1, 1))
+                u_h[rows, columns], u_l[rows, columns] = parts(total)
     send_own(2, 0, low_in.at[0])
     for kind in (2, 1, 0):
         exchange(kind).start()
@@ -470,6 +534,7 @@
         map_ref[child] = index_ref[f if child == 0 else partner, child:child + 1, :]
     if packed:
         pl.loop(0, 2)(tables)
+        fits_out[0] = counts_fit(index_ref, order, width, limits)
 
         @pl.when(middle)
         def _():
@@ -512,13 +577,12 @@
             serve_own(1)
 
         subtract(0, blocks // 2, blocks)
-        inner(1, 2, middle)
+        take_late()
         subtract(1, 0, blocks)
+        last_update()
         for k in range(2):
             hand_on(k).start()
-        inner(1, 3, at_end)
-        hand_on(2).start()
-        for k in range(3):
+        for k in range(2):
             hand_on(k).wait()
     else:
         relay_low(0, 1)
@@ -552,16 +616,20 @@
             serve_all(child)
             serve_own(child)
             subtract(child, 0, blocks)
-        for k in range(2):
+        for k, ref in enumerate((u_h, u_l)):
+            ref[...] = jnp.zeros_like(ref)
             hand_on(k).start()
             hand_on(k).wait()
+        fits_out[0] = 1
 
     for child in range(2):
         @pl.loop(0, n)
         def _(s):
             for side in range(2):
                 for kind in range(3):
-                    @pl.when(takes(kind, side) & (s <= t if side == 0 else s >= t))
+                    whole = ~(middle & (s == late)) if packed and (kind, child) == (2, 1) else t >= 0
+
+                    @pl.when(takes(kind, side) & (s <= t if side == 0 else s >= t) & whole)
                     def _():
                         hop(kind, child, s, side).wait_send()
 
@@ -580,10 +648,11 @@
             def _():
                 cross_copy(child).wait_send()
 
-    if not packed:
-        low[1, late] = jnp.zeros(late_out.shape, jnp.float32)
-        hand_on(2).start()
-        hand_on(2).wait()
+            @pl.when(server)
+            def _():
+                if child == 1:
+                    for k in range(2):
+                        late_copy(k, aside).wait_send()
 
 
 def capacity(draws, share, order):
@@ -627,16 +696,16 @@
             vmem((cross_pad, pivots), b16),
             vmem((cap_pad, pivots), b16),
             vmem((cap_pad, pivots), b16),
-            dma((2,)), dma((2,)),
+            dma((2,)), dma((2,)), dma((2,)), dma((2,)),
         ]
     whole = pl.BlockSpec(memory_space=pl.ANY)
     return pl.pallas_call(
         functools.partial(front_kernel, n, limits),
         out_shape=[jax.ShapeDtypeStruct((order, width), f32)]
-        + [jax.ShapeDtypeStruct((width, pivots), b16)] * 2
-        + [jax.ShapeDtypeStruct((lr, pivots), f32)],
+        + [jax.ShapeDtypeStruct((lr, width), b16)] * 2
+        + [jax.ShapeDtypeStruct((1,), jnp.int32)],
         in_specs=[whole] * 3 + [pl.BlockSpec(memory_space=vmem), whole],
-        out_specs=[whole] * 4,
+        out_specs=[whole] * 3 + [pl.BlockSpec(memory_space=pltpu.SMEM)],
         scratch_shapes=[
             vmem((2, 1, count), jnp.int32),
             vmem((2, held, pivots, wc), f32),
@@ -653,13 +722,15 @@
             vmem(f_shape, f32),
             vmem((2, width, pivots), b16),
             vmem((2, width, pivots), b16),
+            vmem((lr, width), b16),
+            vmem((lr, width), b16),
             vmem((slots, min(1024, order), chunk), f32),
             dma((3,)), dma((3,)), dma((3,)),
             dma((2, 2, n)), dma((2, n)),
             dma((2, 2, n)), dma((2, n)),
             dma((2, 2, n)), dma((2, n)),
             dma(f_sems), dma(f_sems),
-            dma((slots,)), dma((slots,)), dma((3,)),
+            dma((slots,)), dma((slots,)), dma((2,)),
         ] + extra,
         compiler_params=pltpu.CompilerParams(
             collective_id=int(packed), has_side_effects=True, vmem_limit_bytes=63 * 1024 * 1024
@@ -668,14 +739,14 @@
 
 
 def finish_kernel(
-    n, index_ref, x_in, last_h, last_l, late_in, out,
-    x_buf, f_h, f_l, late, u_h, u_l, x_sem, out_sem, f_sem,
+    n, index_ref, x_in, u_h_in, u_l_in, out,
+    x_buf, u_h, u_l, x_sem, out_sem, u_sem,
 ):
     t = lax.axis_index("tile")
     f = lax.axis_index("front")
     partner = lax.rem(f, 2) * -2 + 1 + f
     slots, rows, width = x_buf.shape
-    lr = late.shape[0]
+    lr = u_h.shape[0]
     blocks = out.shape[0] // rows
     ahead = slots // 2
     chunk = min(256, width)
@@ -694,22 +765,15 @@
         return pltpu.make_async_copy(x_buf.at[slot], out.at[window(i)], out_sem.at[slot])
 
     first = [
-        pltpu.make_async_copy(source, target, f_sem.at[k])
-        for k, (source, target) in enumerate(((late_in, late), (last_h, f_h), (last_l, f_l)))
+        pltpu.make_async_copy(source, target, u_sem.at[k])
+        for k, (source, target) in enumerate(((u_h_in, u_h), (u_l_in, u_l)))
     ]
     for copy in first:
         copy.start()
+    for i in range(min(ahead, blocks)):
+        load(i).start()
     for copy in first:
         copy.wait()
-    for i in range(min(ahead, blocks)):
-        load(i).start()
-    left = parts(late[...])
-    for j in range(width // chunk):
-        columns = slice(j * chunk, (j + 1) * chunk)
-        total = dot(left[0], f_h[columns, :], (1, 1))
-        total = total + dot(left[0], f_l[columns, :], (1, 1))
-        total = total + dot(left[1], f_h[columns, :], (1, 1))
-        u_h[:, columns], u_l[:, columns] = parts(total)
 
     @pl.loop(0, blocks)
     def _(i):
@@ -734,40 +798,24 @@
         store(i).wait()
 
 
-def finished(n, index_map, x, f_h, f_l, late):
+def finished(n, index_map, x, u_h, u_l):
     order, width = x.shape
-    rows, slots = min(512, order), 4
+    rows, slots = min(512, order), 6
     vmem, dma, b16 = pltpu.VMEM, pltpu.SemaphoreType.DMA, jnp.bfloat16
     whole = pl.BlockSpec(memory_space=pl.ANY)
     return pl.pallas_call(
         functools.partial(finish_kernel, n),
         out_shape=jax.ShapeDtypeStruct(x.shape, x.dtype),
-        in_specs=[pl.BlockSpec(memory_space=vmem)] + [whole] * 4,
+        in_specs=[pl.BlockSpec(memory_space=vmem)] + [whole] * 3,
         out_specs=whole,
         scratch_shapes=[
             vmem((slots, rows, width), x.dtype),
-            vmem(f_h.shape, b16),
-            vmem(f_h.shape, b16),
-            vmem(late.shape, late.dtype),
-            vmem((late.shape[0], width), b16),
-            vmem((late.shape[0], width), b16),
-            dma((slots,)), dma((slots,)), dma((3,)),
+            vmem(u_h.shape, b16),
+            vmem(u_h.shape, b16),
+            dma((slots,)), dma((slots,)), dma((2,)),
         ],
         compiler_params=pltpu.CompilerParams(vmem_limit_bytes=60 * 1024 * 1024),
-    )(index_map, x, f_h, f_l, late)
-
-
-def fits_kernel(ranges, index_ref, out_ref):
-    index = index_ref[...]
-    early = lax.broadcasted_iota(jnp.int32, index.shape, 2) < index.shape[2] // 2
-    over = None
-    for start, stop, is_early, limit in ranges:
-        inside = (index >= start) & (index < stop)
-        if is_early is not None:
-            inside &= early if is_early else ~early
-        extra = jnp.sum(inside.astype(jnp.int32), axis=2, keepdims=True) - limit
-        over = extra if over is None else jnp.maximum(over, extra)
-    out_ref[0] = (jnp.max(over) <= 0).astype(jnp.int32)
+    )(index_map, x, u_h, u_l)
 
 
 def shards(pivot_inverse, panel_upper, panel_lower, index_map, parent_base):
@@ -784,23 +832,14 @@
     def run(limits, *args):
         return tuple(assembled(*args, n, limits))
 
+    def whole_transfers():
+        return finished(n, index_map, *run(None, *operands)[:3])
+
     if n != 4 or total >= width or cross >= count // 2:
-        return finished(n, index_map, *run(None, *operands))[None]
-
-    ranges = (
-        (side, order, True, cross), (0, side, False, cross),
-        (0, width, None, total), (0, width, False, far),
-        (order - width, order, None, total), (order - width, order, True, far),
-    )
-    fits = pl.pallas_call(
-        functools.partial(fits_kernel, ranges),
-        out_shape=jax.ShapeDtypeStruct((1,), jnp.int32),
-        in_specs=[pl.BlockSpec(memory_space=pltpu.VMEM)],
-        out_specs=pl.BlockSpec(memory_space=pltpu.SMEM),
-    )(index_map)
-    return finished(n, index_map, *lax.cond(
-        fits[0] > 0, functools.partial(run, (total, far, cross)), functools.partial(run, None), *operands
-    ))[None]
+        return whole_transfers()[None]
+
+    x, u_h, u_l, fits = run((total, far, cross), *operands)
+    return lax.cond(fits[0] > 0, lambda: finished(n, index_map, x, u_h, u_l), whole_transfers)[None]
 
 
 def solution(mesh):

time: 215 us -> 212 us (0.986)
  Pallas kernels: 214 us -> 211 us
    pallas_call x1, Pallas kernels: 16.7 us -> 14.5 us  [finished(): pl.pallas_call(functools.partial(finish_kernel, n), out_shape=jax.ShapeDt...]
where the time goes in v7:
time: 212 us
  Pallas kernels  211 us (100%)
    pallas_call x1, Pallas kernels, assembled(): pl.pallas_call(functools.partial(front_kernel, n, limits), out_shape=[jax...  197 us
    pallas_call x1, Pallas kernels, finished(): pl.pallas_call(functools.partial(finish_kernel, n), out_shape=jax.ShapeDt...  14.5 us

profile of v7, /device:TPU:0, one launch (start us, length us, event | category | flops | bytes accessed | tf_op | source)
XLA Modules:
  0.0 212.2 jit_solution(13678689712211130632)
XLA Ops:
  0.0 0.0 copy-start
  0.0 0.0 copy-start.1
  0.0 196.9 %shard_map.57 = (f32[4096,1024]{1,0:T(8,128)}, bf16[512,1024]{1,0:T(8,128)(2,1)}, bf16[512,1024]{1,0:T(8,128)(2,1)}, s32[1]{0:T(128)}) custom-call(f32[2,128,512]{2,1,0:T(8,128)} %bitcast.15, f32[2,512,512]{2,1,0:T(8,128)} %bitcast.11, f32[2,512,512]{2,1,0:T(8,128)} %bitcast.13, s32[8,2,2048]{2,1,0:T(2,128)} %index_ref.1, f32[4096,1024]{1,0:T(8,128)} %bitcast.7), custom_call_target="tpu_custom_call" | custom-call | tf_op jit(solution)/shard_map/pallas_call | solution.py:702
  197.4 0.0 copy-done
  197.5 0.0 copy-done.1
  197.5 14.5 %conditional.1 = (f32[1,4096,1024]{2,1,0:T(8,128)}) conditional(s32[]{:T(128)} %bitcast.6, (f32[2,128,512]{2,1,0:T(8,128)S(1)}, f32[2,512,512]{2,1,0:T(8,128)}, f32[2,512,512]{2,1,0:T(8,128)}, s32[8,2,2048]{2,1,0:T(2,128)S(1)}, f32[4096,1024]{1,0:T(8,128)}) %tuple.24, (s32[8,2,2048]{2,1,0:T(2,128)S(1)}, f32[4096,1024]{1,0:T(8,128)}, ...), branch_computations={%region_0.0_spmd, %region_1.0_spmd} | conditional | bytes 8 | solution.py:842
  197.5 14.5 %branch_1_fun.1 = f32[4096,1024]{1,0:T(8,128)} custom-call(s32[8,2,2048]{2,1,0:T(2,128)S(1)} %get-tuple-element.35.index_ref, f32[4096,1024]{1,0:T(8,128)} %get-tuple-element.36.x_in, bf16[512,1024]{1,0:T(8,128)(2,1)} %get-tuple-element.37.u_h_in, bf16[512,1024]{1,0:T(8,128)(2,1)} %get-tuple-element.38.u_l_in), custom_call_target="tpu_custom_call" | custom-call | tf_op jit(solution)/shard_map/cond/branch_1_fun/pallas_call | solution.py:806
Async XLA Ops:
  0.0 197.4 %copy-start = (s32[8,2,2048]{2,1,0:T(2,128)S(1)}, s32[8,2,2048]{2,1,0:T(2,128)}, u32[]{:S(2)}) copy-start(s32[8,2,2048]{2,1,0:T(2,128)} %index_ref.1) | copy-start | bytes 393220
  0.0 197.5 %copy-start.1 = (f32[1,2,128,512]{3,2,1,0:T(8,128)S(1)}, f32[1,2,128,512]{3,2,1,0:T(8,128)}, u32[]{:S(2)}) copy-start(f32[1,2,128,512]{3,2,1,0:T(8,128)} %param.7) | copy-start | bytes 1572868

commit v8 on v7

--- a/solution.py
+++ b/solution.py
@@ -14,14 +14,6 @@
 def parts(value):
     high = value.astype(jnp.bfloat16)
     return high, (value - high.astype(jnp.float32)).astype(jnp.bfloat16)
-
-
-def spread(value, targets):
-    rows = value.shape[0]
-    for ref, part in zip(targets, parts(value)):
-        ref[:rows] = part
-        if rows < ref.shape[0]:
-            ref[rows:] = jnp.zeros((ref.shape[0] - rows, ref.shape[1]), jnp.bfloat16)
 
 
 def dot(left, right, contract=(1, 0)):
@@ -390,21 +382,35 @@
             def _(j):
                 keep(child, j, factor(child, range_of(t * width + j * chunk)))
 
+    def expand(child, begin, stop, stop_pad):
+        value = f_buf[child, begin:stop]
+        for ref, part in zip((g_h, g_l), parts(value)):
+            ref[begin:stop] = part
+            if stop < stop_pad:
+                ref[stop:stop_pad] = jnp.zeros((stop_pad - stop, ref.shape[1]), jnp.bfloat16)
+
+        @pl.loop(0, chunks)
+        def _(j):
+            choose = one_hot(range_of(t * width + j * chunk) == row_want[child, :, begin:stop_pad])
+            for ref, source in ((f_h, g_h), (f_l, g_l)):
+                found = dot(choose, source[begin:stop_pad, :]).astype(jnp.bfloat16)
+                ref[child, strip(j), :] = found if begin == 0 else ref[child, strip(j), :] + found
+
+    def take_first(child):
+        @pl.when(at_end)
+        def _():
+            end_copy(child, 0, aside).wait_recv()
+            expand(child, 0, split // 128 * 128, split // 128 * 128)
+
     def take_factor(child):
         @pl.when(at_end)
         def _():
             if packed:
-                for q in range(2):
-                    end_copy(child, q, aside).wait_recv()
-                spread(f_buf[child], (g_h, g_l))
-
-            @pl.loop(0, chunks)
-            def _(j):
-                if packed:
-                    choose = one_hot(range_of(t * width + j * chunk) == row_want[child])
-                    for ref, source in ((f_h, g_h), (f_l, g_l)):
-                        ref[child, strip(j), :] = dot(choose, source[...]).astype(jnp.bfloat16)
-                else:
+                end_copy(child, 1, aside).wait_recv()
+                expand(child, split // 128 * 128, total_cap, g_h.shape[0])
+            else:
+                @pl.loop(0, chunks)
+                def _(j):
                     end_copy(child, j, aside).wait_recv()
                     keep(child, j, f_buf[child, j])
 
@@ -418,16 +424,20 @@
         rows = pl.ds(pl.multiple_of(lax.rem(i, per) * tall, tall), tall)
         return ref.at[rows, strip(lax.div(i, per))]
 
+    def store(i):
+        slot = lax.rem(i, slots)
+        return pltpu.make_async_copy(x_buf.at[slot], window(x_out, i), out_sem.at[slot])
+
+    def settle(begin, stop):
+        for i in range(max(stop - slots, begin), stop):
+            store(i).wait()
+
     def subtract(child, begin, stop):
         source = base_in if child == 0 else x_out
 
         def load(i):
             slot = lax.rem(i, slots)
             return pltpu.make_async_copy(window(source, i), x_buf.at[slot], in_sem.at[slot])
-
-        def store(i):
-            slot = lax.rem(i, slots)
-            return pltpu.make_async_copy(x_buf.at[slot], window(x_out, i), out_sem.at[slot])
 
         for i in range(begin, min(begin + ahead, stop)):
             load(i).start()
@@ -457,11 +467,10 @@
             x_buf[slot] = x_buf[slot] - total
             store(i).start()
 
-        for i in range(max(stop - slots, begin), stop):
-            store(i).wait()
-
-    def hand_on(k):
-        return pltpu.make_async_copy((u_h, u_l)[k], (u_h_out, u_l_out)[k], out_copy_sem.at[k])
+    def hand_on(k, q):
+        return pltpu.make_async_copy(
+            (u_h, u_l)[k].at[late_rows(q)], (u_h_out, u_l_out)[k].at[late_rows(q)], out_copy_sem.at[k, q]
+        )
 
     late = jnp.where(lower, n - 1, 0)
 
@@ -507,6 +516,12 @@
                 total = total + dot(left[0], f_l[1, columns, :], (1, 1))
                 total = total + dot(left[1], f_h[1, columns, :], (1, 1))
                 u_h[rows, columns], u_l[rows, columns] = parts(total)
+
+            for q in range(2):
+                @pl.when(k == q)
+                def _():
+                    for m in range(2):
+                        hand_on(m, q).start()
     send_own(2, 0, low_in.at[0])
     for kind in (2, 1, 0):
         exchange(kind).start()
@@ -569,7 +584,9 @@
             far(1)
             serve_near(1)
 
+        take_first(0)
         subtract(0, 0, blocks // 2)
+        settle(0, blocks // 2)
 
         @pl.when(middle)
         def _():
@@ -577,13 +594,15 @@
             serve_own(1)
 
         subtract(0, blocks // 2, blocks)
+        settle(blocks // 2, blocks)
+        take_first(1)
         take_late()
         subtract(1, 0, blocks)
         last_update()
-        for k in range(2):
-            hand_on(k).start()
-        for k in range(2):
-            hand_on(k).wait()
+        settle(0, blocks)
+        for m in range(2):
+            for q in range(2):
+                hand_on(m, q).wait()
     else:
         relay_low(0, 1)
         relay_low(1, 1)
@@ -616,10 +635,12 @@
             serve_all(child)
             serve_own(child)
             subtract(child, 0, blocks)
-        for k, ref in enumerate((u_h, u_l)):
+            settle(0, blocks)
+        for m, ref in enumerate((u_h, u_l)):
             ref[...] = jnp.zeros_like(ref)
-            hand_on(k).start()
-            hand_on(k).wait()
+            for q in range(2):
+                hand_on(m, q).start()
+                hand_on(m, q).wait()
         fits_out[0] = 1
 
     for child in range(2):
@@ -730,7 +751,7 @@
             dma((2, 2, n)), dma((2, n)),
             dma((2, 2, n)), dma((2, n)),
             dma(f_sems), dma(f_sems),
-            dma((slots,)), dma((slots,)), dma((2,)),
+            dma((slots,)), dma((slots,)), dma((2, 2)),
         ] + extra,
         compiler_params=pltpu.CompilerParams(
             collective_id=int(packed), has_side_effects=True, vmem_limit_bytes=63 * 1024 * 1024
@@ -835,7 +856,7 @@
     def whole_transfers():
         return finished(n, index_map, *run(None, *operands)[:3])
 
-    if n != 4 or total >= width or cross >= count // 2:
+    if n != 4 or total >= width or total - far < 128 or cross >= count // 2:
         return whole_transfers()[None]
 
     x, u_h, u_l, fits = run((total, far, cross), *operands)

time: 212 us -> 212 us (level)
  no operation moved by 1% of the time
where the time goes in v8:
time: 212 us
  Pallas kernels  211 us (100%)
    pallas_call x1, Pallas kernels, assembled(): pl.pallas_call(functools.partial(front_kernel, n, limits), out_shape=[jax...  197 us
    pallas_call x1, Pallas kernels, finished(): pl.pallas_call(functools.partial(finish_kernel, n), out_shape=jax.ShapeDt...  14.5 us

profile of v8, /device:TPU:0, one launch (start us, length us, event | category | flops | bytes accessed | tf_op | source)
XLA Modules:
  0.0 211.8 jit_solution(8528057822690431786)
XLA Ops:
  0.0 0.0 copy-start
  0.0 0.0 copy-start.1
  0.0 196.5 %shard_map.57 = (f32[4096,1024]{1,0:T(8,128)}, bf16[512,1024]{1,0:T(8,128)(2,1)}, bf16[512,1024]{1,0:T(8,128)(2,1)}, s32[1]{0:T(128)}) custom-call(f32[2,128,512]{2,1,0:T(8,128)} %bitcast.15, f32[2,512,512]{2,1,0:T(8,128)} %bitcast.11, f32[2,512,512]{2,1,0:T(8,128)} %bitcast.13, s32[8,2,2048]{2,1,0:T(2,128)} %index_ref.1, f32[4096,1024]{1,0:T(8,128)} %bitcast.7), custom_call_target="tpu_custom_call" | custom-call | tf_op jit(solution)/shard_map/pallas_call | solution.py:723
  197.1 0.0 copy-done
  197.1 0.0 copy-done.1
  197.1 14.5 %conditional.1 = (f32[1,4096,1024]{2,1,0:T(8,128)}) conditional(s32[]{:T(128)} %bitcast.6, (f32[2,128,512]{2,1,0:T(8,128)S(1)}, f32[2,512,512]{2,1,0:T(8,128)}, f32[2,512,512]{2,1,0:T(8,128)}, s32[8,2,2048]{2,1,0:T(2,128)S(1)}, f32[4096,1024]{1,0:T(8,128)}) %tuple.24, (s32[8,2,2048]{2,1,0:T(2,128)S(1)}, f32[4096,1024]{1,0:T(8,128)}, ...), branch_computations={%region_0.0_spmd, %region_1.0_spmd} | conditional | bytes 8 | solution.py:863
  197.1 14.5 %branch_1_fun.1 = f32[4096,1024]{1,0:T(8,128)} custom-call(s32[8,2,2048]{2,1,0:T(2,128)S(1)} %get-tuple-element.35.index_ref, f32[4096,1024]{1,0:T(8,128)} %get-tuple-element.36.x_in, bf16[512,1024]{1,0:T(8,128)(2,1)} %get-tuple-element.37.u_h_in, bf16[512,1024]{1,0:T(8,128)(2,1)} %get-tuple-element.38.u_l_in), custom_call_target="tpu_custom_call" | custom-call | tf_op jit(solution)/shard_map/cond/branch_1_fun/pallas_call | solution.py:827
Async XLA Ops:
  0.0 197.1 %copy-start = (s32[8,2,2048]{2,1,0:T(2,128)S(1)}, s32[8,2,2048]{2,1,0:T(2,128)}, u32[]{:S(2)}) copy-start(s32[8,2,2048]{2,1,0:T(2,128)} %index_ref.1) | copy-start | bytes 393220
  0.0 197.1 %copy-start.1 = (f32[1,2,128,512]{3,2,1,0:T(8,128)S(1)}, f32[1,2,128,512]{3,2,1,0:T(8,128)}, u32[]{:S(2)}) copy-start(f32[1,2,128,512]{3,2,1,0:T(8,128)} %param.7) | copy-start | bytes 1572868

commit v9 on v8

--- a/solution.py
+++ b/solution.py
@@ -791,10 +791,11 @@
     ]
     for copy in first:
         copy.start()
-    for i in range(min(ahead, blocks)):
-        load(i).start()
+    load(0).start()
     for copy in first:
         copy.wait()
+    for i in range(1, min(ahead, blocks)):
+        load(i).start()
 
     @pl.loop(0, blocks)
     def _(i):

time: 212 us -> 211 us (level)
  no operation moved by 1% of the time
where the time goes in v9:
time: 211 us
  Pallas kernels  210 us (100%)
    pallas_call x1, Pallas kernels, assembled(): pl.pallas_call(functools.partial(front_kernel, n, limits), out_shape=[jax...  197 us
    pallas_call x1, Pallas kernels, finished(): pl.pallas_call(functools.partial(finish_kernel, n), out_shape=jax.ShapeDt...  13.9 us

profile of v9, /device:TPU:0, one launch (start us, length us, event | category | flops | bytes accessed | tf_op | source)
XLA Modules:
  0.0 211.2 jit_solution(2109219166556685165)
XLA Ops:
  0.0 0.0 copy-start
  0.0 0.0 copy-start.1
  0.0 196.5 %shard_map.57 = (f32[4096,1024]{1,0:T(8,128)}, bf16[512,1024]{1,0:T(8,128)(2,1)}, bf16[512,1024]{1,0:T(8,128)(2,1)}, s32[1]{0:T(128)}) custom-call(f32[2,128,512]{2,1,0:T(8,128)} %bitcast.15, f32[2,512,512]{2,1,0:T(8,128)} %bitcast.11, f32[2,512,512]{2,1,0:T(8,128)} %bitcast.13, s32[8,2,2048]{2,1,0:T(2,128)} %index_ref.1, f32[4096,1024]{1,0:T(8,128)} %bitcast.7), custom_call_target="tpu_custom_call" | custom-call | tf_op jit(solution)/shard_map/pallas_call | solution.py:723
  197.1 0.0 copy-done
  197.1 0.0 copy-done.1
  197.1 13.9 %conditional.1 = (f32[1,4096,1024]{2,1,0:T(8,128)}) conditional(s32[]{:T(128)} %bitcast.6, (f32[2,128,512]{2,1,0:T(8,128)S(1)}, f32[2,512,512]{2,1,0:T(8,128)}, f32[2,512,512]{2,1,0:T(8,128)}, s32[8,2,2048]{2,1,0:T(2,128)S(1)}, f32[4096,1024]{1,0:T(8,128)}) %tuple.24, (s32[8,2,2048]{2,1,0:T(2,128)S(1)}, f32[4096,1024]{1,0:T(8,128)}, ...), branch_computations={%region_0.0_spmd, %region_1.0_spmd} | conditional | bytes 8 | solution.py:864
  197.1 13.9 %branch_1_fun.1 = f32[4096,1024]{1,0:T(8,128)} custom-call(s32[8,2,2048]{2,1,0:T(2,128)S(1)} %get-tuple-element.35.index_ref, f32[4096,1024]{1,0:T(8,128)} %get-tuple-element.36.x_in, bf16[512,1024]{1,0:T(8,128)(2,1)} %get-tuple-element.37.u_h_in, bf16[512,1024]{1,0:T(8,128)(2,1)} %get-tuple-element.38.u_l_in), custom_call_target="tpu_custom_call" | custom-call | tf_op jit(solution)/shard_map/cond/branch_1_fun/pallas_call | solution.py:828
Async XLA Ops:
  0.0 197.1 %copy-start = (s32[8,2,2048]{2,1,0:T(2,128)S(1)}, s32[8,2,2048]{2,1,0:T(2,128)}, u32[]{:S(2)}) copy-start(s32[8,2,2048]{2,1,0:T(2,128)} %index_ref.1) | copy-start | bytes 393220
  0.0 197.1 %copy-start.1 = (f32[1,2,128,512]{3,2,1,0:T(8,128)S(1)}, f32[1,2,128,512]{3,2,1,0:T(8,128)}, u32[]{:S(2)}) copy-start(f32[1,2,128,512]{3,2,1,0:T(8,128)} %param.7) | copy-start | bytes 1572868
